TPU v7x, 32 devices: a whole 2x2x4 slice. The times are simulated.
32 devices in a mesh: bias: 2 (over x), ea: 16 (over z, y, core).
Axes of the slice: x: 2, y: 2, z: 4, core: 2. Of those that a mesh axis runs over, the one named last changes fastest.
Arguments:
- g_lesser: bfloat16 [512, 2, 256, 256], P(('bias', 'ea')), parts along dimension 0, may hold values from -6 to 6
- g_greater: bfloat16 [512, 2, 256, 256], P(('bias', 'ea')), parts along dimension 0, may hold values from -6 to 6
- g_free: bfloat16 [512, 2, 256, 256], P(('bias', 'ea')), parts along dimension 0, may hold values from -3 to 3
- coulomb: bfloat16 [256, 256], replicated, may hold values from -0.375 to 0.375
Outputs:
- g_new: bfloat16 [512, 2, 256, 256], P(('bias', 'ea')), parts along dimension 0
There are 2 independent parts, one for each index of `bias`. A program takes and returns all parts, laid end to end along the dimension named above; an argument that names none is the same for every part. Nothing has to cross between parts.
All inputs are finite; a program needn't handle non-finite values.
Results may differ from a plain program's by a relative error of at most 0.022.
Values may be sent and summed in bfloat16 or wider, within the bound.
No kernel may reach another device: no remote copies, remote signals or barrier semaphores. Data moves between devices by JAX's collectives and lax.ppermute only.
A program may use at most 192 MiB of HBM per device.

v0:
```python
import math

import jax
import jax.numpy as jnp
from jax import lax
from jax.sharding import PartitionSpec as P

NE = 256


def dft_tables(length, count):
    freq = jnp.arange(length, dtype=jnp.int32)
    places = jnp.arange(count, dtype=jnp.int32)
    phase = freq[:, None] * places[None, :] % length
    angle = phase.astype(jnp.float32) * (2.0 * math.pi / length)
    cosine = jnp.cos(angle)
    sine = jnp.sin(angle)
    stacked = jnp.concatenate([cosine, sine], axis=0)
    upper = stacked.astype(jnp.bfloat16)
    lower = (stacked - upper.astype(jnp.float32)).astype(jnp.bfloat16)
    backward = jnp.concatenate([cosine.T, sine.T], axis=0)
    return (upper, lower, backward)


def forward(tables, block, sign):
    upper, lower = tables
    length = upper.shape[0] // 2
    real_part = block[:, 0].reshape(block.shape[0], -1)
    imag_part = block[:, 1].reshape(block.shape[0], -1)
    width = real_part.shape[1]
    joined = jnp.concatenate([real_part, imag_part], axis=1)
    result = jnp.dot(upper, joined, preferred_element_type=jnp.float32)
    result = result + jnp.dot(lower, joined, preferred_element_type=jnp.float32)
    cos_real = result[:length, :width]
    cos_imag = result[:length, width:]
    sin_real = result[length:, :width]
    sin_imag = result[length:, width:]
    return (cos_real - sign * sin_imag, cos_imag + sign * sin_real)


def inverse(backward, real_part, imag_part, scale):
    count = backward.shape[0] // 2
    width = real_part.shape[1]
    joined = jnp.concatenate([real_part, imag_part], axis=1)
    result = jnp.dot(
        backward, joined, precision=lax.Precision.HIGH, preferred_element_type=jnp.float32
    )
    cos_real = result[:count, :width]
    cos_imag = result[:count, width:]
    sin_real = result[count:, :width]
    sin_imag = result[count:, width:]
    return ((cos_real - sin_imag) * scale, (cos_imag + sin_real) * scale)


def complex_mul(left, right):
    return (left[0] * right[0] - left[1] * right[1], left[0] * right[1] + left[1] * right[0])


def restack(real_part, imag_part, shape):
    return jnp.stack([real_part.reshape(shape), imag_part.reshape(shape)], axis=1).astype(
        jnp.bfloat16
    )


def batched(left, right):
    return jnp.einsum("eij,ejk->eik", left, right, preferred_element_type=jnp.float32)


def per_device(g_lesser, g_greater, g_free, coulomb):
    length = 2 * NE
    upper, lower, backward = dft_tables(length, NE)
    tables = (upper, lower)
    scale = 1.0 / (length * NE)
    greater_t = jnp.swapaxes(g_greater, 2, 3)
    lesser_rows, greater_rows = (
        lax.all_to_all(g_lesser, "ea", split_axis=2, concat_axis=0, tiled=True),
        lax.all_to_all(greater_t, "ea", split_axis=2, concat_axis=0, tiled=True),
    )
    spec_lesser = forward(tables, lesser_rows, -1.0)
    element_shape = (NE, lesser_rows.shape[2], lesser_rows.shape[3])
    spec_greater = forward(tables, greater_rows, 1.0)
    joined = complex_mul(spec_lesser, spec_greater)
    polar_real, polar_imag = inverse(backward, joined[0], joined[1], scale)
    polar_rows = restack(polar_real, polar_imag, element_shape)
    polar = lax.all_to_all(polar_rows, "ea", split_axis=0, concat_axis=2, tiled=True)
    mixed_real = jnp.einsum(
        "eij,jk->eik", polar[:, 0], coulomb, preferred_element_type=jnp.float32
    ).astype(jnp.bfloat16)
    mixed_imag = jnp.einsum(
        "eij,jk->eik", polar[:, 1], coulomb, preferred_element_type=jnp.float32
    ).astype(jnp.bfloat16)
    square_real = batched(mixed_real, mixed_real) - batched(mixed_imag, mixed_imag)
    square_imag = batched(mixed_real, mixed_imag) + batched(mixed_imag, mixed_real)
    inner_real = (mixed_real.astype(jnp.float32) + square_real).astype(jnp.bfloat16)
    inner_imag = (mixed_imag.astype(jnp.float32) + square_imag).astype(jnp.bfloat16)
    screen_real = coulomb.astype(jnp.float32)[None] + jnp.einsum(
        "ij,ejk->eik", coulomb, inner_real, preferred_element_type=jnp.float32
    )
    screen_imag = jnp.einsum("ij,ejk->eik", coulomb, inner_imag, preferred_element_type=jnp.float32)
    screen = jnp.stack([screen_real, screen_imag], axis=1).astype(jnp.bfloat16)
    screen_rows = lax.all_to_all(screen, "ea", split_axis=2, concat_axis=0, tiled=True)
    spec_screen = forward(tables, screen_rows, -1.0)
    folded = complex_mul(spec_lesser, spec_screen)
    sigma_real, sigma_imag = inverse(backward, folded[0], folded[1], scale)
    sigma_rows = restack(sigma_real, sigma_imag, element_shape)
    sigma = lax.all_to_all(sigma_rows, "ea", split_axis=0, concat_axis=2, tiled=True)
    free_real = g_free[:, 0]
    free_imag = g_free[:, 1]
    right_real = (batched(sigma[:, 0], free_real) - batched(sigma[:, 1], free_imag)).astype(
        jnp.bfloat16
    )
    right_imag = (batched(sigma[:, 0], free_imag) + batched(sigma[:, 1], free_real)).astype(
        jnp.bfloat16
    )
    out_real = (
        free_real.astype(jnp.float32)
        + batched(free_real, right_real)
        - batched(free_imag, right_imag)
    )
    out_imag = (
        free_imag.astype(jnp.float32)
        + batched(free_real, right_imag)
        + batched(free_imag, right_real)
    )
    return jnp.stack([out_real, out_imag], axis=1).astype(jnp.bfloat16)


def solution(mesh):
    return jax.shard_map(
        per_device,
        mesh=mesh,
        in_specs=(
            P(("bias", "ea"), None, None, None),
            P(("bias", "ea"), None, None, None),
            P(("bias", "ea"), None, None, None),
            P(),
        ),
        out_specs=P(("bias", "ea"), None, None, None),
        check_vma=False,
    )
```

profile of v0, /device:TPU:1, one launch (start us, length us, event | category | flops | bytes accessed | tf_op | source)
XLA Modules:
  0.0 771.9 jit_solution(499210198396497137)
XLA Ops:
  0.0 11.1 %copy.96 = bf16[16,2,256,256]{2,1,0,3:T(2,128)(2,1)} copy(bf16[16,2,256,256]{3,2,1,0:T(8,128)(2,1)} %param.5) | data formatting | bytes 8388608 | tf_op args[1]
  11.1 7.3 all-to-all-start.1
  18.5 6.5 copy.92
  25.0 71.6 %all-to-all-done.1 = bf16[16,2,256,256]{3,1,0,2:T(2,128)(2,1)} async-done(((bf16[16,2,256,256]{3,1,0,2:T(2,128)(2,1)}), bf16[16,2,256,256]{3,1,0,2:T(2,128)(2,1)}, u32[]{:S(2)}, u32[]{:S(2)}) %all-to-all-start.1) | async-done | bytes 4194336 | tf_op jit(solution)/shard_map/all_to_all | solution.py:77
  96.6 19.8 %all-to-all-start = ((bf16[16,2,256,256]{3,0,1,2:T(8,128)(2,1)}), bf16[16,2,256,256]{3,0,1,2:T(8,128)(2,1)}, u32[]{:S(2)}, u32[]{:S(2)}) async-start(bf16[16,2,256,256]{3,0,1,2:T(8,128)(2,1)} %copy.92), calls=%async_computation | async-start | bytes 8388608 | tf_op jit(solution)/shard_map/all_to_all | solution.py:76
  118.5 2.9 fusion.69
  121.4 4.6 copy.97
  129.3 13.1 %fusion.79 = f32[1024,8192]{1,0:T(8,128)} fusion(bf16[256,8192]{1,0:T(8,128)(2,1)S(1)} %constant_dynamic-update-slice_fusion.2, f32[512,256]{1,0:T(8,128)S(1)} %get-tuple-element.20, f32[512,256]{1,0:T(8,128)S(1)} %get-tuple-element.21), kind=kOutput, calls=%fused_computation.124 | convolution fusion | flops 4296015872 | bytes 38797312 | tf_op jit(solution)/shard_map/dot_general | solution.py:32
  142.5 25.0 %convolution_add_fusion.1 = f32[1024,8192]{1,0:T(8,128)} fusion(f32[1024,8192]{1,0:T(8,128)} %fusion.79, bf16[256,8192]{1,0:T(8,128)(2,1)S(1)} %constant_dynamic-update-slice_fusion.2, f32[512,256]{1,0:T(8,128)S(1)} %get-tuple-element.20, f32[512,256]{1,0:T(8,128)} %copy-done.2), kind=kOutput, calls=%fused_computation.1 | convolution fusion | flops 4304666624 | bytes 72351744 | tf_op jit(solution)/shard_map/dot_general | solution.py:33
  167.5 26.9 %all-to-all-done = bf16[16,2,256,256]{3,0,1,2:T(8,128)(2,1)} async-done(((bf16[16,2,256,256]{3,0,1,2:T(8,128)(2,1)}), bf16[16,2,256,256]{3,0,1,2:T(8,128)(2,1)}, u32[]{:S(2)}, u32[]{:S(2)}) %all-to-all-start) | async-done | bytes 4194336 | tf_op jit(solution)/shard_map/all_to_all | solution.py:76
  194.4 5.0 copy.94
  202.1 13.1 %fusion.81 = f32[1024,8192]{1,0:T(8,128)} fusion(bf16[256,8192]{1,0:T(8,128)(2,1)S(1)} %constant_dynamic-update-slice_fusion, f32[512,256]{1,0:T(8,128)S(1)} %get-tuple-element.20, f32[512,256]{1,0:T(8,128)S(1)} %copy-done.3), kind=kOutput, calls=%fused_computation.125 | convolution fusion | flops 4296015872 | bytes 38797312 | tf_op jit(solution)/shard_map/dot_general | solution.py:32
  215.2 24.9 %convolution_add_fusion.2 = f32[1024,8192]{1,0:T(8,128)} fusion(f32[1024,8192]{1,0:T(8,128)} %fusion.81, bf16[256,8192]{1,0:T(8,128)(2,1)S(1)} %constant_dynamic-update-slice_fusion, f32[512,256]{1,0:T(8,128)S(1)} %get-tuple-element.20, f32[512,256]{1,0:T(8,128)} %copy-done.2), kind=kOutput, calls=%fused_computation.2 | convolution fusion | flops 4304666624 | bytes 72351744 | tf_op jit(solution)/shard_map/dot_general | solution.py:33
  240.0 31.5 %multiply_subtract_fusion.1 = (f32[512,4096]{1,0:T(8,128)}, f32[512,4096]{1,0:T(8,128)}, f32[512,4096]{1,0:T(8,128)}) fusion(f32[1024,8192]{1,0:T(8,128)} %convolution_add_fusion.1, f32[1024,8192]{1,0:T(8,128)} %convolution_add_fusion.2), kind=kLoop, calls=%fused_computation.24 | loop fusion | flops 18874368 | bytes 92274688 | tf_op jit(solution)/shard_map/sub | solution.py:56
  271.5 22.0 %multiply_add_fusion.1 = f32[512,4096]{1,0:T(8,128)} fusion(f32[512,4096]{1,0:T(8,128)} %get-tuple-element.7, f32[512,4096]{1,0:T(8,128)} %get-tuple-element.6, f32[1024,8192]{1,0:T(8,128)} %convolution_add_fusion.1), kind=kLoop, calls=%fused_computation.23 | loop fusion | flops 10485760 | bytes 58720256 | tf_op jit(solution)/shard_map/add | solution.py:56
  293.6 19.5 %fusion = f32[512,8192]{1,0:T(8,128)} fusion(f32[512,4096]{1,0:T(8,128)} %multiply_add_fusion.1, f32[512,4096]{1,0:T(8,128)} %get-tuple-element.5, f32[256,512]{1,0:T(8,128)S(1)} %copy-done.6, f32[256,512]{1,0:T(8,128)S(1)} %copy-done.8), kind=kOutput, calls=%fused_computation.3 | convolution fusion | flops 12889358336 | bytes 34603008 | tf_op jit(solution)/shard_map/dot_general | solution.py:45
  313.1 6.7 fusion.19
  323.5 19.2 %all-to-all-start.2 = ((bf16[256,2,16,256]{3,2,1,0:T(8,128)(2,1)}), bf16[256,2,16,256]{3,2,1,0:T(8,128)(2,1)}, u32[]{:S(2)}, u32[]{:S(2)}) async-start(bf16[256,2,16,256]{3,2,1,0:T(8,128)(2,1)} %pad_maximum_fusion), calls=%async_computation.2 | async-start | bytes 8388608 | tf_op jit(solution)/shard_map/all_to_all | solution.py:85
  342.8 78.0 %all-to-all-done.2 = bf16[256,2,16,256]{3,2,1,0:T(8,128)(2,1)} async-done(((bf16[256,2,16,256]{3,2,1,0:T(8,128)(2,1)}), bf16[256,2,16,256]{3,2,1,0:T(8,128)(2,1)}, u32[]{:S(2)}, u32[]{:S(2)}) %all-to-all-start.2) | async-done | bytes 4194336 | tf_op jit(solution)/shard_map/all_to_all | solution.py:85
  427.7 2.8 fusion.89
  430.5 6.4 convert_bitcast_fusion
  436.8 6.4 fusion.42
  443.3 4.6 pad_maximum_fusion.1
  447.9 7.9 %copy.104 = bf16[16,2,256,256]{3,0,1,2:T(8,128)(2,1)} copy(bf16[16,2,256,256]{2,3,0,1:T(8,128)(2,1)} %pad_maximum_fusion.1) | data formatting | bytes 8388608 | tf_op jit(solution)/shard_map/stack | solution.py:100
  455.8 111.9 %all_to_all.90 = bf16[16,2,256,256]{3,0,1,2:T(8,128)(2,1)S(1)} all-to-all(bf16[16,2,256,256]{3,0,1,2:T(8,128)(2,1)} %copy.104), channel_id=1, replica_groups=mesh['bias'=2,'ea'=16] {'ea'}, dimensions={2} | all-to-all | bytes 8388608 | tf_op jit(solution)/shard_map/all_to_all | solution.py:101
  567.7 2.9 copy.106
  573.3 13.1 %fusion.77 = f32[1024,8192]{1,0:T(8,128)} fusion(bf16[256,8192]{1,0:T(8,128)(2,1)S(1)} %constant_dynamic-update-slice_fusion.4, f32[512,256]{1,0:T(8,128)S(1)} %get-tuple-element.20, f32[512,256]{1,0:T(8,128)S(1)} %copy-done.4), kind=kOutput, calls=%fused_computation.123 | convolution fusion | flops 4296015872 | bytes 38797312 | tf_op jit(solution)/shard_map/dot_general | solution.py:32
  586.4 24.8 %convolution_add_fusion = f32[1024,8192]{1,0:T(8,128)} fusion(f32[1024,8192]{1,0:T(8,128)} %fusion.77, bf16[256,8192]{1,0:T(8,128)(2,1)S(1)} %constant_dynamic-update-slice_fusion.4, f32[512,256]{1,0:T(8,128)S(1)} %get-tuple-element.20, f32[512,256]{1,0:T(8,128)} %copy-done.2), kind=kOutput, calls=%fused_computation | convolution fusion | flops 4304666624 | bytes 72351744 | tf_op jit(solution)/shard_map/dot_general | solution.py:33
  611.2 23.8 %multiply_subtract_fusion = (f32[512,4096]{1,0:T(8,128)}, f32[512,4096]{1,0:T(8,128)}) fusion(f32[512,4096]{1,0:T(8,128)} %get-tuple-element.7, f32[512,4096]{1,0:T(8,128)} %get-tuple-element.6, f32[1024,8192]{1,0:T(8,128)} %convolution_add_fusion), kind=kLoop, calls=%fused_computation.22 | loop fusion | flops 20971520 | bytes 67108864 | tf_op jit(solution)/shard_map/sub | solution.py:56
  635.1 19.7 %fusion.4 = f32[512,8192]{1,0:T(8,128)} fusion(f32[512,4096]{1,0:T(8,128)} %get-tuple-element.9, f32[512,4096]{1,0:T(8,128)} %get-tuple-element.8, f32[256,512]{1,0:T(8,128)S(1)} %copy-done.7, f32[256,512]{1,0:T(8,128)S(1)} %copy-done.9), kind=kOutput, calls=%fused_computation.7 | convolution fusion | flops 12889358336 | bytes 34603008 | tf_op jit(solution)/shard_map/dot_general | solution.py:45
  654.8 6.7 fusion.15
  663.1 97.5 %all_to_all.91 = bf16[256,2,16,256]{3,2,1,0:T(8,128)(2,1)S(1)} all-to-all(bf16[256,2,16,256]{3,2,1,0:T(8,128)(2,1)S(1)} %pad_maximum_fusion.2), channel_id=1, replica_groups=mesh['bias'=2,'ea'=16] {'ea'}, dimensions={0} | all-to-all | bytes 8388608 | tf_op jit(solution)/shard_map/all_to_all | solution.py:106
  (59 shorter events, 33.9 us)
Async XLA Ops:
  11.1 85.5 %all-to-all-start.1 = ((bf16[16,2,256,256]{3,1,0,2:T(2,128)(2,1)}), bf16[16,2,256,256]{3,1,0,2:T(2,128)(2,1)}, u32[]{:S(2)}, u32[]{:S(2)}) async-start(bf16[16,2,256,256]{3,1,0,2:T(2,128)(2,1)} %bitcast.181), calls=%async_computation.1 | async-start | bytes 8388608 | tf_op jit(solution)/shard_map/all_to_all | solution.py:77
  96.6 97.8 %all-to-all-start = ((bf16[16,2,256,256]{3,0,1,2:T(8,128)(2,1)}), bf16[16,2,256,256]{3,0,1,2:T(8,128)(2,1)}, u32[]{:S(2)}, u32[]{:S(2)}) async-start(bf16[16,2,256,256]{3,0,1,2:T(8,128)(2,1)} %copy.92), calls=%async_computation | async-start | bytes 8388608 | tf_op jit(solution)/shard_map/all_to_all | solution.py:76
  118.5 10.9 %copy-start.2 = (f32[512,256]{1,0:T(8,128)}, f32[512,256]{1,0:T(8,128)S(1)}, u32[]{:S(2)}) copy-start(f32[512,256]{1,0:T(8,128)S(1)} %get-tuple-element.21) | copy-start | bytes 1572868
  200.9 1.2 copy-start.3
  271.5 22.0 %copy-start.6 = (f32[256,512]{1,0:T(8,128)S(1)}, f32[256,512]{1,0:T(8,128)}, u32[]{:S(2)}) copy-start(f32[256,512]{1,0:T(8,128)} %get-tuple-element.22) | copy-start | bytes 1572868
  271.5 22.0 %copy-start.8 = (f32[256,512]{1,0:T(8,128)S(1)}, f32[256,512]{1,0:T(8,128)}, u32[]{:S(2)}) copy-start(f32[256,512]{1,0:T(8,128)} %get-tuple-element.23) | copy-start | bytes 1572868
  323.5 19.2 %copy-start.5 = (bf16[256,256]{1,0:T(8,128)(2,1)S(1)}, bf16[256,256]{1,0:T(8,128)(2,1)}, u32[]{:S(2)}) copy-start(bf16[256,256]{1,0:T(8,128)(2,1)} %param.7) | copy-start | bytes 393220
  323.5 97.4 %all-to-all-start.2 = ((bf16[256,2,16,256]{3,2,1,0:T(8,128)(2,1)}), bf16[256,2,16,256]{3,2,1,0:T(8,128)(2,1)}, u32[]{:S(2)}, u32[]{:S(2)}) async-start(bf16[256,2,16,256]{3,2,1,0:T(8,128)(2,1)} %pad_maximum_fusion), calls=%async_computation.2 | async-start | bytes 8388608 | tf_op jit(solution)/shard_map/all_to_all | solution.py:85
  425.0 2.7 copy-start.1
  572.1 1.2 copy-start.4
  611.2 23.8 %copy-start.7 = (f32[256,512]{1,0:T(8,128)S(1)}, f32[256,512]{1,0:T(8,128)}, u32[]{:S(2)}) copy-start(f32[256,512]{1,0:T(8,128)} %get-tuple-element.22) | copy-start | bytes 1572868
  611.2 23.8 %copy-start.9 = (f32[256,512]{1,0:T(8,128)S(1)}, f32[256,512]{1,0:T(8,128)}, u32[]{:S(2)}) copy-start(f32[256,512]{1,0:T(8,128)} %get-tuple-element.23) | copy-start | bytes 1572868
  760.6 2.2 copy-start
where the time goes:
time: 776 us; the launch traced here: 772 us
  blocking collectives  209 us (27%)
  matrix products  179 us (23%)
  waiting for transfers between devices  177 us (23%)
  other arithmetic  103 us (13%)
  local copies, waits for them, and re-layouts  56.6 us (7%)
  starting transfers between devices  46.3 us (6%)
    all_to_all x1, blocking collectives, per_device(): lax.all_to_all(screen, 'ea', split_axis=2, concat_axis=0, tiled=True)  112 us
    all_to_all x1, blocking collectives, per_device(): lax.all_to_all(sigma_rows, 'ea', split_axis=0, concat_axis=2, tiled=True)  97.5 us
    all_to_all x1, waiting for transfers between devices, per_device(): lax.all_to_all(polar_rows, 'ea', split_axis=0, concat_axis=2, tiled=True)  78 us
    dot_general x3, matrix products, forward(): result = result + jnp.dot(lower, joined, preferred_element_type=jnp.float32)  74.7 us
    all_to_all x1, waiting for transfers between devices, per_device(): lax.all_to_all(greater_t, 'ea', split_axis=2, concat_axis=0, tiled=True)  71.6 us
    sub x2, other arithmetic, complex_mul(): left[0] * right[0] - left[1] * right[1]  55.3 us
    dot_general x3, matrix products, forward(): result = jnp.dot(upper, joined, preferred_element_type=jnp.float32)  39.4 us
    dot_general x2, matrix products, inverse(): jnp.dot(backward, joined, precision=lax.Precision.HIGH, preferred_element...  39.3 us
  transfers between devices with their start and end apart: 3, of which 3 were waited for; matrix products, arithmetic and copies ran while one was open for 7% of the time, Pallas kernels for 0%

commit v1 on v0

--- a/solution.py
+++ b/solution.py
@@ -1,11 +1,278 @@
+import functools
 import math
 
 import jax
 import jax.numpy as jnp
 from jax import lax
+from jax.experimental import pallas as pl
+from jax.experimental.pallas import tpu as pltpu
 from jax.sharding import PartitionSpec as P
 
-NE = 256
+BF = jnp.bfloat16
+F32 = jnp.float32
+
+
+def dot(left, right):
+    return jnp.dot(left, right, preferred_element_type=F32)
+
+
+def swap_matrix(block):
+    size = block * block
+    row = lax.broadcasted_iota(jnp.int32, (size, size), 0)
+    col = lax.broadcasted_iota(jnp.int32, (size, size), 1)
+    return ((row % block) * block + row // block == col).astype(BF)
+
+
+def spectral_tables(count):
+    length = 2 * count
+    freq = jnp.arange(length, dtype=jnp.int32)
+    places = jnp.arange(count, dtype=jnp.int32)
+    angle = (freq[:, None] * places[None, :] % length).astype(F32) * (2.0 * math.pi / length)
+    cosine, sine = jnp.cos(angle), jnp.sin(angle)
+
+    def joined(sign):
+        top = jnp.concatenate([cosine, -sign * sine], axis=1)
+        return jnp.concatenate([top, jnp.concatenate([sign * sine, cosine], axis=1)], axis=0)
+
+    forward = joined(-1.0)
+    return (
+        forward.astype(BF),
+        joined(1.0).astype(BF),
+        (forward.T * (1.0 / (length * count))).astype(BF),
+    )
+
+
+def pack_rows_kernel(swap_ref, in_ref, out_ref):
+    block = in_ref.shape[0]
+    size = in_ref.shape[-1]
+    for j in range(out_ref.shape[0]):
+        piece = in_ref[:, 0, block * j : block * (j + 1), :].reshape(block * block, size)
+        out_ref[j, 0] = dot(swap_ref[...], piece).astype(BF).reshape(block, block, size)
+
+
+def pack_rows(swap, g):
+    block, _, size, _ = g.shape
+    groups = size // block
+    per = 4
+    return pl.pallas_call(
+        pack_rows_kernel,
+        grid=(2, groups // per),
+        in_specs=[
+            pl.BlockSpec(swap.shape, lambda r, j: (0, 0)),
+            pl.BlockSpec((block, 1, block * per, size), lambda r, j: (0, r, j, 0)),
+        ],
+        out_specs=pl.BlockSpec((per, 1, block, block, size), lambda r, j: (j, r, 0, 0, 0)),
+        out_shape=jax.ShapeDtypeStruct((groups, 2, block, block, size), BF),
+        cost_estimate=pl.CostEstimate(
+            flops=4 * block * size**3, bytes_accessed=4 * g.size, transcendentals=0
+        ),
+        name="pack_rows",
+    )(swap, g)
+
+
+def pack_columns_kernel(swap_ref, eye_ref, in_ref, out_ref, turned):
+    block = in_ref.shape[0]
+    size = in_ref.shape[2]
+    for e in range(block):
+        turned[e] = lax.dot_general(
+            eye_ref[...], in_ref[e, 0], (((1,), (1,)), ((), ())), preferred_element_type=F32
+        ).astype(BF)
+    for j in range(out_ref.shape[0]):
+        piece = turned[:, block * j : block * (j + 1), :].reshape(block * block, size)
+        out_ref[j, 0] = dot(swap_ref[...], piece).astype(BF).reshape(block, block, size)
+
+
+def pack_columns(swap, g):
+    block, _, size, _ = g.shape
+    groups = size // block
+    lanes = 128
+    per = lanes // block
+    eye = jnp.eye(lanes, dtype=BF)
+    return pl.pallas_call(
+        pack_columns_kernel,
+        grid=(2, size // lanes),
+        in_specs=[
+            pl.BlockSpec(swap.shape, lambda r, j: (0, 0)),
+            pl.BlockSpec(eye.shape, lambda r, j: (0, 0)),
+            pl.BlockSpec((block, 1, size, lanes), lambda r, j: (0, r, 0, j)),
+        ],
+        out_specs=pl.BlockSpec((per, 1, block, block, size), lambda r, j: (j, r, 0, 0, 0)),
+        out_shape=jax.ShapeDtypeStruct((groups, 2, block, block, size), BF),
+        scratch_shapes=[pltpu.VMEM((block, lanes, size), BF)],
+        cost_estimate=pl.CostEstimate(
+            flops=8 * block * size**3, bytes_accessed=4 * g.size, transcendentals=0
+        ),
+        name="pack_columns",
+    )(swap, eye, g)
+
+
+def stacked(ref):
+    size = ref.shape[-1]
+    return jnp.concatenate(
+        [ref[:, 0, 0].reshape(-1, size), ref[:, 1, 0].reshape(-1, size)], axis=0
+    )
+
+
+def unstack(out_ref, value):
+    count = value.shape[0] // 2
+    shape = (out_ref.shape[0],) + out_ref.shape[3:]
+    value = value.astype(BF)
+    out_ref[:, 0, 0] = value[:count].reshape(shape)
+    out_ref[:, 1, 0] = value[count:].reshape(shape)
+
+
+def product(left, right):
+    half = left.shape[0] // 2
+    lr, li = left[:half], left[half:]
+    rr, ri = right[:half], right[half:]
+    return jnp.concatenate([lr * rr - li * ri, lr * ri + li * rr], axis=0).astype(BF)
+
+
+def polar_kernel(minus_ref, plus_ref, back_ref, lesser_ref, greater_ref, out_ref, spec_ref):
+    spec_lesser = dot(minus_ref[...], stacked(lesser_ref))
+    spec_ref[0] = spec_lesser.astype(BF)
+    spec_greater = dot(plus_ref[...], stacked(greater_ref))
+    unstack(out_ref, dot(back_ref[...], product(spec_lesser, spec_greater)))
+
+
+def fold_kernel(minus_ref, back_ref, spec_ref, screen_ref, out_ref):
+    spec_screen = dot(minus_ref[...], stacked(screen_ref))
+    unstack(out_ref, dot(back_ref[...], product(spec_ref[0].astype(F32), spec_screen)))
+
+
+def whole_spec(array):
+    return pl.BlockSpec(array.shape, lambda *_: (0,) * array.ndim)
+
+
+def row_spec(array):
+    shape = array.shape
+    return pl.BlockSpec((shape[0], 2, 1) + shape[3:], lambda a: (0, 0, a, 0, 0))
+
+
+def polarization(tables, lesser, greater):
+    minus, plus, back = tables
+    rows, size = lesser.shape[2], lesser.shape[4]
+    spec_shape = (rows, minus.shape[0], size)
+    return pl.pallas_call(
+        polar_kernel,
+        grid=(rows,),
+        in_specs=[whole_spec(minus), whole_spec(plus), whole_spec(back), row_spec(lesser), row_spec(greater)],
+        out_specs=[row_spec(lesser), pl.BlockSpec((1,) + spec_shape[1:], lambda a: (a, 0, 0))],
+        out_shape=[
+            jax.ShapeDtypeStruct(lesser.shape, BF),
+            jax.ShapeDtypeStruct(spec_shape, BF),
+        ],
+        cost_estimate=pl.CostEstimate(
+            flops=6 * rows * minus.size * size,
+            bytes_accessed=6 * lesser.size + 2 * rows * minus.shape[0] * size,
+            transcendentals=0,
+        ),
+        name="polarization",
+    )(minus, plus, back, lesser, greater)
+
+
+def self_energy(tables, spec, screen):
+    minus, _, back = tables
+    rows, size = screen.shape[2], screen.shape[4]
+    return pl.pallas_call(
+        fold_kernel,
+        grid=(rows,),
+        in_specs=[
+            whole_spec(minus),
+            whole_spec(back),
+            pl.BlockSpec((1,) + spec.shape[1:], lambda a: (a, 0, 0)),
+            row_spec(screen),
+        ],
+        out_specs=row_spec(screen),
+        out_shape=jax.ShapeDtypeStruct(screen.shape, BF),
+        cost_estimate=pl.CostEstimate(
+            flops=4 * rows * minus.size * size,
+            bytes_accessed=4 * screen.size + 2 * spec.size,
+            transcendentals=0,
+        ),
+        name="self_energy",
+    )(minus, back, spec, screen)
+
+
+def gather_matrices(swap_ref, in_ref, whole):
+    block, size = in_ref.shape[2], in_ref.shape[4]
+
+    @pl.loop(0, in_ref.shape[0])
+    def _(s):
+        for r in range(2):
+            piece = in_ref[s, r].reshape(block * block, size)
+            whole[r, :, s] = dot(swap_ref[...], piece).astype(BF).reshape(block, block, size)
+
+
+def screen_kernel(swap_ref, coulomb_ref, in_ref, out_ref, whole):
+    size = coulomb_ref.shape[0]
+    block = in_ref.shape[2]
+    gather_matrices(swap_ref, in_ref, whole)
+    volts = coulomb_ref[...]
+
+    @pl.loop(0, block)
+    def _(w):
+        mr = dot(whole[0, w].reshape(size, size), volts).astype(BF)
+        mi = dot(whole[1, w].reshape(size, size), volts).astype(BF)
+        nr = (mr.astype(F32) + (dot(mr, mr) - dot(mi, mi))).astype(BF)
+        ni = (mi.astype(F32) + (dot(mr, mi) + dot(mi, mr))).astype(BF)
+        wr = (volts.astype(F32) + dot(volts, nr)).astype(BF)
+        wi = dot(volts, ni).astype(BF)
+        whole[0, w] = wr.reshape(whole.shape[2:])
+        whole[1, w] = wi.reshape(whole.shape[2:])
+
+    @pl.loop(0, in_ref.shape[0])
+    def _(d):
+        for r in range(2):
+            piece = whole[r, :, d].reshape(block * block, size)
+            out_ref[d, r] = dot(swap_ref[...], piece).astype(BF).reshape(block, block, size)
+
+
+def screened(swap, coulomb, polar):
+    groups, _, block, _, size = polar.shape
+    return pl.pallas_call(
+        screen_kernel,
+        out_shape=jax.ShapeDtypeStruct(polar.shape, BF),
+        scratch_shapes=[pltpu.VMEM((2, block, groups, block, size), BF)],
+        cost_estimate=pl.CostEstimate(
+            flops=20 * block * size**3, bytes_accessed=4 * polar.size, transcendentals=0
+        ),
+        name="screened",
+    )(swap, coulomb, polar)
+
+
+def dyson_kernel(swap_ref, sigma_ref, free_ref, out_ref, whole):
+    size = free_ref.shape[-1]
+    e = pl.program_id(0)
+
+    @pl.when(e == 0)
+    def _():
+        gather_matrices(swap_ref, sigma_ref, whole)
+
+    sr = whole[0, e].reshape(size, size)
+    si = whole[1, e].reshape(size, size)
+    fr, fi = free_ref[0, 0], free_ref[0, 1]
+    rr = (dot(sr, fr) - dot(si, fi)).astype(BF)
+    ri = (dot(sr, fi) + dot(si, fr)).astype(BF)
+    out_ref[0, 0] = (fr.astype(F32) + dot(fr, rr) - dot(fi, ri)).astype(BF)
+    out_ref[0, 1] = (fi.astype(F32) + dot(fr, ri) + dot(fi, rr)).astype(BF)
+
+
+def dyson(swap, sigma, free):
+    groups, _, block, _, size = sigma.shape
+    energy_spec = pl.BlockSpec((1, 2, size, size), lambda e: (e, 0, 0, 0))
+    return pl.pallas_call(
+        dyson_kernel,
+        grid=(block,),
+        in_specs=[whole_spec(swap), whole_spec(sigma), energy_spec],
+        out_specs=energy_spec,
+        out_shape=jax.ShapeDtypeStruct(free.shape, BF),
+        scratch_shapes=[pltpu.VMEM((2, block, groups, block, size), BF)],
+        cost_estimate=pl.CostEstimate(
+            flops=18 * block * size**3, bytes_accessed=6 * free.size, transcendentals=0
+        ),
+        name="dyson",
+    )(swap, sigma, free)
 
 
 def dft_tables(length, count):
@@ -66,18 +333,19 @@
     return jnp.einsum("eij,ejk->eik", left, right, preferred_element_type=jnp.float32)
 
 
-def per_device(g_lesser, g_greater, g_free, coulomb):
-    length = 2 * NE
-    upper, lower, backward = dft_tables(length, NE)
+def plain_device(g_lesser, g_greater, g_free, coulomb):
+    ne = lax.axis_size("ea") * g_lesser.shape[0]
+    length = 2 * ne
+    upper, lower, backward = dft_tables(length, ne)
     tables = (upper, lower)
-    scale = 1.0 / (length * NE)
+    scale = 1.0 / (length * ne)
     greater_t = jnp.swapaxes(g_greater, 2, 3)
     lesser_rows, greater_rows = (
         lax.all_to_all(g_lesser, "ea", split_axis=2, concat_axis=0, tiled=True),
         lax.all_to_all(greater_t, "ea", split_axis=2, concat_axis=0, tiled=True),
     )
     spec_lesser = forward(tables, lesser_rows, -1.0)
-    element_shape = (NE, lesser_rows.shape[2], lesser_rows.shape[3])
+    element_shape = (ne, lesser_rows.shape[2], lesser_rows.shape[3])
     spec_greater = forward(tables, greater_rows, 1.0)
     joined = complex_mul(spec_lesser, spec_greater)
     polar_real, polar_imag = inverse(backward, joined[0], joined[1], scale)
@@ -125,6 +393,25 @@
     return jnp.stack([out_real, out_imag], axis=1).astype(jnp.bfloat16)
 
 
+def exchange(blocks):
+    return lax.all_to_all(blocks, "ea", split_axis=0, concat_axis=0, tiled=True)
+
+
+def per_device(g_lesser, g_greater, g_free, coulomb):
+    block, _, size, _ = g_lesser.shape
+    count = lax.axis_size("ea") * block
+    if block != 16 or size != 16 * lax.axis_size("ea"):
+        return plain_device(g_lesser, g_greater, g_free, coulomb)
+    swap = swap_matrix(block)
+    tables = spectral_tables(count)
+    lesser = exchange(pack_rows(swap, g_lesser))
+    greater = exchange(pack_columns(swap, g_greater))
+    polar, spec = polarization(tables, lesser, greater)
+    screen = exchange(screened(swap, coulomb, exchange(polar)))
+    sigma = exchange(self_energy(tables, spec, screen))
+    return dyson(swap, sigma, g_free)
+
+
 def solution(mesh):
     return jax.shard_map(
         per_device,

time: 776 us -> 595 us (0.77)
  matrix products: 179 us -> 0 us
  Pallas kernels: 0 us -> 110 us
  blocking collectives: 209 us -> 307 us
  other arithmetic: 103 us -> 11.1 us
  local copies, waits for them, and re-layouts: 56.6 us -> 2.65 us
  waiting for transfers between devices: 177 us -> 137 us
  starting transfers between devices: 46.3 us -> 26.4 us
    dot_general x22 -> x0, matrix products: 179 us -> none  [the longest x3 74.7 us: forward(): result = result + jnp.dot(lower, joined, preferred_element_type=jnp.float32)]
    pallas_call x0 -> x6, Pallas kernels: none -> 110 us  [the longest x1 28.8 us: polarization(): pl.pallas_call(polar_kernel, grid=(rows,), in_specs=[whole_spec(minus), w...]
    all_to_all x2 -> x3, blocking collectives: 209 us -> 307 us  [exchange(): return lax.all_to_all(blocks, 'ea', split_axis=0, concat_axis=0, tiled=True)]
    sub x2 -> x0, other arithmetic: 55.3 us -> none  [complex_mul(): left[0] * right[0] - left[1] * right[1]]
    all_to_all x3 -> x2, waiting for transfers between devices: 177 us -> 137 us  [exchange(): return lax.all_to_all(blocks, 'ea', split_axis=0, concat_axis=0, tiled=True)]
    unnamed x35 -> x0, local copies, waits for them, and re-layouts: 28.3 us -> none
    add x1, other arithmetic: 22 us -> 0.01 us  [swap_matrix(): return (row % block * block + row // block == col).astype(BF)]
    all_to_all x3 -> x2, starting transfers between devices: 46.3 us -> 26.4 us  [exchange(): return lax.all_to_all(blocks, 'ea', split_axis=0, concat_axis=0, tiled=True)]
  transfers between devices with their start and end apart: 3 -> 2, of which waited for: 3 -> 2; matrix products, arithmetic and copies ran while one was open for 7% -> 2% of each run, Pallas kernels for 0% -> 1%
where the time goes in v1:
time: 595 us; the launch traced here: 594 us
  blocking collectives  307 us (52%)
  waiting for transfers between devices  137 us (23%)
  Pallas kernels  110 us (18%)
  starting transfers between devices  26.4 us (4%)
  other arithmetic  11.1 us (2%)
    all_to_all x3, blocking collectives, exchange(): return lax.all_to_all(blocks, 'ea', split_axis=0, concat_axis=0, tiled=True)  307 us
    all_to_all x2, waiting for transfers between devices, exchange(): return lax.all_to_all(blocks, 'ea', split_axis=0, concat_axis=0, tiled=True)  137 us
    pallas_call x1, Pallas kernels, polarization(): pl.pallas_call(polar_kernel, grid=(rows,), in_specs=[whole_spec(minus), w...  28.8 us
    all_to_all x2, starting transfers between devices, exchange(): return lax.all_to_all(blocks, 'ea', split_axis=0, concat_axis=0, tiled=True)  26.4 us
    pallas_call x1, Pallas kernels, self_energy(): pl.pallas_call(fold_kernel, grid=(rows,), in_specs=[whole_spec(minus), wh...  24.1 us
    pallas_call x1, Pallas kernels, screened(): pl.pallas_call(screen_kernel, out_shape=jax.ShapeDtypeStruct(polar.shape,...  23.8 us
    pallas_call x1, Pallas kernels, dyson(): pl.pallas_call(dyson_kernel, grid=(block,), in_specs=[whole_spec(swap), w...  19.4 us
  transfers between devices with their start and end apart: 2, of which 2 were waited for; matrix products, arithmetic and copies ran while one was open for 2% of the time, Pallas kernels for 1%

profile of v1, /device:TPU:1, one launch (start us, length us, event | category | flops | bytes accessed | tf_op | source)
XLA Modules:
  0.0 593.9 jit_solution(10301476753789482007)
XLA Ops:
  0.0 0.6 fusion.14.eye_ref
  0.7 0.9 fusion.11.swap_ref
  1.6 6.4 %pack_columns.1 = bf16[16,2,16,16,256]{4,3,2,1,0:T(8,128)(2,1)} custom-call(bf16[256,256]{1,0:T(8,128)(2,1)} %fusion.11.swap_ref, bf16[128,128]{1,0:T(8,128)(2,1)} %fusion.14.eye_ref, bf16[16,2,256,256]{3,2,1,0:T(8,128)(2,1)} %in_ref.3), custom_call_target="tpu_custom_call" | custom-call | flops 2147483648 | bytes 8388608 | tf_op jit(solution)/shard_map/pack_columns/pallas_call | solution.py:91
  8.0 7.3 %all-to-all-start.1 = ((bf16[16,2,16,16,256]{4,3,2,1,0:T(8,128)(2,1)}), bf16[16,2,16,16,256]{4,3,2,1,0:T(8,128)(2,1)}, u32[]{:S(2)}, u32[]{:S(2)}) async-start(bf16[16,2,16,16,256]{4,3,2,1,0:T(8,128)(2,1)} %pack_columns.1), calls=%async_computation.1 | async-start | bytes 8388608 | tf_op jit(solution)/shard_map/all_to_all | solution.py:397
  15.4 7.5 %pack_rows.1 = bf16[16,2,16,16,256]{4,3,2,1,0:T(8,128)(2,1)} custom-call(bf16[256,256]{1,0:T(8,128)(2,1)} %fusion.11.swap_ref, bf16[16,2,256,256]{3,2,1,0:T(8,128)(2,1)} %in_ref.2), custom_call_target="tpu_custom_call" | custom-call | flops 1073741824 | bytes 8388608 | tf_op jit(solution)/shard_map/pack_rows/pallas_call | solution.py:57
  22.9 70.6 %all-to-all-done.1.greater_ref = bf16[16,2,16,16,256]{4,3,2,1,0:T(8,128)(2,1)} async-done(((bf16[16,2,16,16,256]{4,3,2,1,0:T(8,128)(2,1)}), bf16[16,2,16,16,256]{4,3,2,1,0:T(8,128)(2,1)}, u32[]{:S(2)}, u32[]{:S(2)}) %all-to-all-start.1) | async-done | bytes 4194336 | tf_op jit(solution)/shard_map/all_to_all | solution.py:397
  93.5 19.1 %all-to-all-start = ((bf16[16,2,16,16,256]{4,3,2,1,0:T(8,128)(2,1)}), bf16[16,2,16,16,256]{4,3,2,1,0:T(8,128)(2,1)}, u32[]{:S(2)}, u32[]{:S(2)}) async-start(bf16[16,2,16,16,256]{4,3,2,1,0:T(8,128)(2,1)} %pack_rows.1), calls=%async_computation | async-start | bytes 8388608 | tf_op jit(solution)/shard_map/all_to_all | solution.py:397
  112.6 2.0 fusion.13
  114.6 2.2 fusion.10
  116.8 0.1 maximum_maximum_fusion.1
  116.9 1.3 copy.6.plus_ref
  118.2 1.9 fusion.9
  120.1 1.9 broadcast_multiply_fusion
  122.1 0.1 fusion
  122.2 1.3 copy.7.minus_ref
  123.5 1.3 fusion.1.back_ref
  124.8 66.0 %all-to-all-done.lesser_ref = bf16[16,2,16,16,256]{4,3,2,1,0:T(8,128)(2,1)} async-done(((bf16[16,2,16,16,256]{4,3,2,1,0:T(8,128)(2,1)}), bf16[16,2,16,16,256]{4,3,2,1,0:T(8,128)(2,1)}, u32[]{:S(2)}, u32[]{:S(2)}) %all-to-all-start) | async-done | bytes 4194336 | tf_op jit(solution)/shard_map/all_to_all | solution.py:397
  190.8 28.8 %polarization.1 = (bf16[16,2,16,16,256]{4,3,2,1,0:T(8,128)(2,1)}, bf16[16,1024,256]{2,1,0:T(8,128)(2,1)}) custom-call(bf16[1024,512]{1,0:T(8,128)(2,1)} %copy.7.minus_ref, bf16[1024,512]{1,0:T(8,128)(2,1)} %copy.6.plus_ref, bf16[512,1024]{1,0:T(8,128)(2,1)} %fusion.1.back_ref, bf16[16,2,16,16,256]{4,3,2,1,0:T(8,128)(2,1)} %all-to-all-done.lesser_ref, ...), custom_call_target="tpu_custom_call" | custom-call | flops 12884901888 | bytes 20971520 | tf_op jit(solution)/shard_map/polarization/pallas_call | solution.py:156
  219.5 111.8 %all_to_all.25.in_ref = bf16[16,2,16,16,256]{4,3,2,1,0:T(8,128)(2,1)} all-to-all(bf16[16,2,16,16,256]{4,3,2,1,0:T(8,128)(2,1)} %get-tuple-element.8), channel_id=1, replica_groups=mesh['bias'=2,'ea'=16] {'ea'}, dimensions={0} | all-to-all | bytes 8388608 | tf_op jit(solution)/shard_map/all_to_all | solution.py:397
  331.4 23.8 %screened.1 = bf16[16,2,16,16,256]{4,3,2,1,0:T(8,128)(2,1)} custom-call(bf16[256,256]{1,0:T(8,128)(2,1)} %fusion.11.swap_ref, bf16[256,256]{1,0:T(8,128)(2,1)} %coulomb_ref.1, bf16[16,2,16,16,256]{4,3,2,1,0:T(8,128)(2,1)} %all_to_all.25.in_ref), custom_call_target="tpu_custom_call" | custom-call | flops 5368709120 | bytes 8388608 | tf_op jit(solution)/shard_map/screened/pallas_call | solution.py:233
  355.2 97.5 %all_to_all.26.screen_ref = bf16[16,2,16,16,256]{4,3,2,1,0:T(8,128)(2,1)} all-to-all(bf16[16,2,16,16,256]{4,3,2,1,0:T(8,128)(2,1)} %screened.1), channel_id=1, replica_groups=mesh['bias'=2,'ea'=16] {'ea'}, dimensions={0} | all-to-all | bytes 8388608 | tf_op jit(solution)/shard_map/all_to_all | solution.py:397
  452.7 24.1 %self_energy.1 = bf16[16,2,16,16,256]{4,3,2,1,0:T(8,128)(2,1)} custom-call(bf16[1024,512]{1,0:T(8,128)(2,1)} %copy.7.minus_ref, bf16[512,1024]{1,0:T(8,128)(2,1)} %fusion.1.back_ref, bf16[16,1024,256]{2,1,0:T(8,128)(2,1)} %get-tuple-element.7.spec_ref, bf16[16,2,16,16,256]{4,3,2,1,0:T(8,128)(2,1)} %all_to_all.26.screen_ref), custom_call_target="tpu_custom_call" | custom-call | flops 8589934592 | bytes 16777216 | tf_op jit(solution)/shard_map/self_energy/pallas_call | solution.py:177
  476.9 97.5 %all_to_all.27.sigma_ref = bf16[16,2,16,16,256]{4,3,2,1,0:T(8,128)(2,1)} all-to-all(bf16[16,2,16,16,256]{4,3,2,1,0:T(8,128)(2,1)} %self_energy.1), channel_id=1, replica_groups=mesh['bias'=2,'ea'=16] {'ea'}, dimensions={0} | all-to-all | bytes 8388608 | tf_op jit(solution)/shard_map/all_to_all | solution.py:397
  574.4 19.4 %dyson.1 = bf16[16,2,256,256]{3,2,1,0:T(8,128)(2,1)} custom-call(bf16[256,256]{1,0:T(8,128)(2,1)} %fusion.11.swap_ref, bf16[16,2,16,16,256]{4,3,2,1,0:T(8,128)(2,1)} %all_to_all.27.sigma_ref, bf16[16,2,256,256]{3,2,1,0:T(8,128)(2,1)} %free_ref.1), custom_call_target="tpu_custom_call" | custom-call | flops 4831838208 | bytes 12582912 | tf_op jit(solution)/shard_map/dyson/pallas_call | solution.py:264
  (3 shorter events, 0.0 us)
Async XLA Ops:
  8.0 85.5 %all-to-all-start.1 = ((bf16[16,2,16,16,256]{4,3,2,1,0:T(8,128)(2,1)}), bf16[16,2,16,16,256]{4,3,2,1,0:T(8,128)(2,1)}, u32[]{:S(2)}, u32[]{:S(2)}) async-start(bf16[16,2,16,16,256]{4,3,2,1,0:T(8,128)(2,1)} %pack_columns.1), calls=%async_computation.1 | async-start | bytes 8388608 | tf_op jit(solution)/shard_map/all_to_all | solution.py:397
  93.5 97.2 %all-to-all-start = ((bf16[16,2,16,16,256]{4,3,2,1,0:T(8,128)(2,1)}), bf16[16,2,16,16,256]{4,3,2,1,0:T(8,128)(2,1)}, u32[]{:S(2)}, u32[]{:S(2)}) async-start(bf16[16,2,16,16,256]{4,3,2,1,0:T(8,128)(2,1)} %pack_rows.1), calls=%async_computation | async-start | bytes 8388608 | tf_op jit(solution)/shard_map/all_to_all | solution.py:397

commit v2 on v0

--- a/solution.py
+++ b/solution.py
@@ -2,10 +2,392 @@
 
 import jax
 import jax.numpy as jnp
+import numpy as np
 from jax import lax
+from jax.experimental import pallas as pl
+from jax.experimental.pallas import tpu as pltpu
+from jax.sharding import Mesh
 from jax.sharding import PartitionSpec as P
 
-NE = 256
+
+BF = jnp.bfloat16
+F32 = jnp.float32
+ROWS = (4, 4, 4, 4)
+STARTS = (0, 4, 8, 12)
+CHUNKS = len(ROWS)
+VMEM = pl.BlockSpec(memory_space=pltpu.VMEM)
+SMEM = pl.BlockSpec(memory_space=pltpu.SMEM)
+
+
+def dot(left, right):
+    return jnp.dot(left, right, preferred_element_type=F32)
+
+
+def swap_matrix(block):
+    size = block * block
+    row = lax.broadcasted_iota(jnp.int32, (size, size), 0)
+    col = lax.broadcasted_iota(jnp.int32, (size, size), 1)
+    return ((row % block) * block + row // block == col).astype(BF)
+
+
+def spectral_tables(count, own_order, mixed_order):
+    length = 2 * count
+    phase = np.outer(np.arange(length), np.arange(count)) % length
+    angle = phase * (2.0 * np.pi / length)
+    cosine, sine = lax.optimization_barrier(
+        tuple(jnp.asarray(f(angle).astype(np.float32)).astype(BF) for f in (np.cos, np.sin))
+    )
+
+    def joined(pick, sign):
+        c, s = pick(cosine), sign * pick(sine)
+        top = jnp.concatenate([c, -s], axis=1)
+        return jnp.concatenate([top, jnp.concatenate([s, c], axis=1)], axis=0)
+
+    def own(table):
+        width = count // 4
+        return jnp.concatenate(
+            [lax.dynamic_slice_in_dim(table, z * width, width, 1) for z in own_order], axis=1
+        )
+
+    def mixed(table):
+        width = count // len(mixed_order)
+        return jnp.concatenate([table[:, z * width : (z + 1) * width] for z in mixed_order], axis=1)
+
+    minus_own = joined(own, -1.0)
+    minus_all = joined(lambda table: table, -1.0)
+    scale = 1.0 / (length * count)
+    tables = dict(
+        minus_own=minus_own,
+        plus_own=joined(own, 1.0),
+        minus_mixed=joined(mixed, -1.0),
+        back_own=minus_own.T * BF(scale),
+        back_all=minus_all.T * BF(scale),
+    )
+    return lax.optimization_barrier(tables)
+
+
+def whole_spec(array):
+    return pl.BlockSpec(array.shape, lambda *_: (0,) * array.ndim)
+
+
+def tile_owners(rows, rest, block, tile):
+    several = block // rows
+    found = []
+    for k in range(several):
+        owner = tile * several + k
+        found.append((owner // rest % 2, owner // (2 * rest), owner % rest))
+    return found
+
+
+def pack_kernel(swap_ref, pick_ref, lesser_ref, greater_ref, out_ref, turned):
+    block = lesser_ref.shape[0]
+    size = lesser_ref.shape[-1]
+    rest = out_ref.shape[0] // 2
+    rows = out_ref.shape[4]
+    for e in range(block):
+        turned[e] = lax.dot_general(
+            pick_ref[...], greater_ref[e, 0], (((1,), (1,)), ((), ())), preferred_element_type=F32
+        ).astype(BF)
+    for tile in range(rows):
+        part = slice(block * tile, block * (tile + 1))
+        pair = jnp.concatenate(
+            [
+                lesser_ref[:, 0, part, :].reshape(block * block, size),
+                turned[:, part, :].reshape(block * block, size),
+            ],
+            axis=1,
+        )
+        value = dot(swap_ref[...], pair).astype(BF)
+        for k, (x, low, r) in enumerate(tile_owners(rows, rest, block, tile)):
+            piece = value[k * rows * block : (k + 1) * rows * block]
+            for which in range(2):
+                out_ref[x * rest + r, low, which, 0] = piece[
+                    :, which * size : (which + 1) * size
+                ].reshape(rows, block, size)
+
+
+def pack(swap, lesser, greater, chunk):
+    block, _, size, _ = lesser.shape
+    rows, start = ROWS[chunk], STARTS[chunk] * block
+    count = rows * block
+    lanes = 128
+    row = lax.broadcasted_iota(jnp.int32, (count, lanes), 0)
+    col = lax.broadcasted_iota(jnp.int32, (count, lanes), 1)
+    pick = (row + start % lanes == col).astype(BF)
+    half = size // block // 2
+    return pl.pallas_call(
+        pack_kernel,
+        grid=(2,),
+        in_specs=[
+            whole_spec(swap),
+            whole_spec(pick),
+            pl.BlockSpec((block, 1, count, size), lambda r: (0, r, start // count, 0)),
+            pl.BlockSpec((block, 1, size, lanes), lambda r: (0, r, 0, start // lanes)),
+        ],
+        out_specs=pl.BlockSpec(
+            (half, 2, 2, 1, rows, block, size), lambda r: (0, 0, 0, r, 0, 0, 0)
+        ),
+        out_shape=jax.ShapeDtypeStruct((half, 2, 2, 2, rows, block, size), BF),
+        scratch_shapes=[pltpu.VMEM((block, count, size), BF)],
+        cost_estimate=pl.CostEstimate(
+            flops=12 * block * count * size**2,
+            bytes_accessed=8 * block * count * size * 2,
+            transcendentals=0,
+        ),
+        name="pack",
+    )(swap, pick, lesser, greater)
+
+
+def product(left, right):
+    half = left.shape[0] // 2
+    lr, li = left[:half], left[half:]
+    rr, ri = right[:half], right[half:]
+    return jnp.concatenate([lr * rr - li * ri, lr * ri + li * rr], axis=0).astype(BF)
+
+
+PAIR = 2
+
+
+def side_by_side(columns):
+    return jnp.concatenate([jnp.concatenate(pieces, axis=0) for pieces in columns], axis=1)
+
+
+def each_pair(count, body):
+    if count == 1:
+        body(0)
+    else:
+        pl.loop(0, count)(body)
+
+
+def polar_kernel(minus_ref, plus_ref, back_ref, *refs):
+    ins, (out_ref, spec_ref) = refs[:4], refs[4:]
+    rows, _, size = ins[0].shape[3:]
+
+    def pair(i):
+        def stacked(k):
+            return side_by_side(
+                [
+                    [ref[:, k, r, i * PAIR + a].reshape(-1, size) for r in range(2) for ref in ins]
+                    for a in range(PAIR)
+                ]
+            )
+
+        spec_lesser = dot(minus_ref[...], stacked(0))
+        spec_ref[i] = spec_lesser.astype(BF)
+        spec_greater = dot(plus_ref[...], stacked(1))
+        value = dot(back_ref[...], product(spec_lesser, spec_greater)).astype(BF)
+        count = value.shape[0] // 2
+        for a in range(PAIR):
+            for r in range(2):
+                piece = value[count * r : count * (r + 1), a * size : (a + 1) * size]
+                out_ref[:, r, i * PAIR + a] = piece.reshape(-1, *out_ref.shape[3:])
+
+    each_pair(rows // PAIR, pair)
+
+
+def polarization(tables, blocks):
+    minus, plus, back = tables["minus_own"], tables["plus_own"], tables["back_all"]
+    rest, _, _, rows, block, size = blocks[0].shape
+    return pl.pallas_call(
+        polar_kernel,
+        in_specs=[VMEM] * 7,
+        out_specs=[VMEM] * 2,
+        out_shape=[
+            jax.ShapeDtypeStruct((4 * rest, 2, rows, block, size), BF),
+            jax.ShapeDtypeStruct((rows // PAIR, minus.shape[0], PAIR * size), BF),
+        ],
+        cost_estimate=pl.CostEstimate(
+            flops=6 * rows * minus.size * size,
+            bytes_accessed=12 * blocks[0].size + 2 * rows * minus.shape[0] * size,
+            transcendentals=0,
+        ),
+        name="polarization",
+    )(minus, plus, back, *blocks)
+
+
+def fold_kernel(place_ref, minus_ref, back_ref, spec_ref, screen_ref, *outs):
+    rows, _, size = screen_ref.shape[3:]
+    half, low = place_ref[0], place_ref[1]
+
+    def pair(i):
+        stacked = side_by_side(
+            [
+                [screen_ref[:, :, r, i * PAIR + a].reshape(-1, size) for r in range(2)]
+                for a in range(PAIR)
+            ]
+        )
+        spec_screen = dot(minus_ref[...], stacked)
+        value = dot(back_ref[...], product(spec_ref[i].astype(F32), spec_screen)).astype(BF)
+        count = value.shape[0] // 8
+        shape = outs[1].shape[:1] + outs[1].shape[3:]
+        for a in range(PAIR):
+            for r in range(2):
+                for k, ref in enumerate(outs):
+                    start = count * (4 * r + k)
+                    piece = value[start : start + count, a * size : (a + 1) * size].reshape(shape)
+                    if k == 0:
+                        ref[half, :, low, r, i * PAIR + a] = piece
+                    else:
+                        ref[:, r, i * PAIR + a] = piece
+
+    each_pair(rows // PAIR, pair)
+
+
+def self_energy(place, tables, spec, screen):
+    minus, back = tables["minus_mixed"], tables["back_own"]
+    both, _, _, rows, block, size = screen.shape
+    rest = both // 2
+    return pl.pallas_call(
+        fold_kernel,
+        in_specs=[SMEM] + [VMEM] * 4,
+        out_specs=[VMEM] * 4,
+        out_shape=[jax.ShapeDtypeStruct((2, rest, 2, 2, rows, block, size), BF)]
+        + [jax.ShapeDtypeStruct((rest, 2, rows, block, size), BF)] * 3,
+        cost_estimate=pl.CostEstimate(
+            flops=4 * rows * minus.size * size,
+            bytes_accessed=4 * screen.size + 2 * spec.size,
+            transcendentals=0,
+        ),
+        name="self_energy",
+    )(place, minus, back, spec, screen)
+
+
+def to_matrices(swap_ref, whole, tile, pieces):
+    block, size = whole.shape[-2:]
+    value = dot(swap_ref[...], jnp.concatenate(pieces, axis=1)).astype(BF)
+    for r in range(2):
+        whole[:, r, tile] = value[:, r * size : (r + 1) * size].reshape(block, block, size)
+
+
+def from_matrices(swap_ref, whole, tile):
+    block, size = whole.shape[-2:]
+    pair = [whole[:, r, tile].reshape(block * block, size) for r in range(2)]
+    value = dot(swap_ref[...], jnp.concatenate(pair, axis=1)).astype(BF)
+    return value[:, :size], value[:, size:]
+
+
+def each_tile(rows, rest, block, body):
+    if rows * rest == block:
+        pl.loop(0, rows, unroll=2)(
+            lambda tile: body(tile, [(tile % 2, tile // 2, r) for r in range(rest)])
+        )
+    else:
+        for tile in range(rows):
+            body(tile, tile_owners(rows, rest, block, tile))
+
+
+def gather_matrices(swap_ref, refs, whole, rest, order):
+    block, size = whole.shape[-2:]
+
+    for ref, start in zip(refs, STARTS):
+
+        def body(tile, owners, ref=ref, start=start):
+            pieces = [
+                jnp.concatenate([ref[(*order(o), r)].reshape(-1, size) for o in owners], axis=0)
+                for r in range(2)
+            ]
+            to_matrices(swap_ref, whole, start + tile, pieces)
+
+        each_tile(ref.shape[-3], rest, block, body)
+
+
+def screen_kernel(place_ref, swap_ref, coulomb_ref, *refs):
+    ins, owns, aways = refs[:CHUNKS], refs[CHUNKS : 2 * CHUNKS], refs[2 * CHUNKS : 3 * CHUNKS]
+    whole = refs[-1]
+    size = coulomb_ref.shape[0]
+    block = whole.shape[-2]
+    rest = ins[0].shape[0] // 4
+    low = place_ref[1]
+    gather_matrices(swap_ref, ins, whole, rest, lambda o: ((o[0] * 2 + o[1]) * rest + o[2],))
+    volts = coulomb_ref[...]
+
+    @pl.loop(0, block, unroll=2)
+    def _(w):
+        mixed = dot(whole[w].reshape(2 * size, size), volts).astype(BF)
+        both = dot(mixed, jnp.concatenate([mixed[:size], mixed[size:]], axis=1))
+        by_real, by_imag = both[:, :size], both[:, size:]
+        nr = (mixed[:size].astype(F32) + (by_real[:size] - by_imag[size:])).astype(BF)
+        ni = (mixed[size:].astype(F32) + (by_imag[:size] + by_real[size:])).astype(BF)
+        pair = dot(volts, jnp.concatenate([nr, ni], axis=1))
+        whole[w, 0] = (volts.astype(F32) + pair[:, :size]).astype(BF).reshape(whole.shape[2:])
+        whole[w, 1] = pair[:, size:].astype(BF).reshape(whole.shape[2:])
+
+    for own_ref, away_ref, start in zip(owns, aways, STARTS):
+        rows = own_ref.shape[3]
+        each = rows // 2
+
+        def tile(t, own_ref=own_ref, away_ref=away_ref, start=start, rows=rows, each=each):
+            width = block // rows
+            for k in range(2):
+                value = from_matrices(swap_ref, whole, start + (low ^ k) * each + t)
+                for r in range(2):
+                    piece = value[r].reshape(width, rows, block, size)
+                    for i in range(width):
+                        if k == 0:
+                            own_ref[t * width + i, low, r] = piece[i]
+                        else:
+                            away_ref[t * width + i, r] = piece[i]
+
+        each_pair(each, tile)
+
+
+def screened(place, swap, coulomb, polar):
+    groups, _, _, block, size = polar[0].shape
+    both = groups // 2
+    return pl.pallas_call(
+        screen_kernel,
+        in_specs=[SMEM] + [VMEM] * (2 + CHUNKS),
+        out_specs=[VMEM] * (2 * CHUNKS),
+        out_shape=[jax.ShapeDtypeStruct((both, 2, 2, rows, block, size), BF) for rows in ROWS]
+        + [jax.ShapeDtypeStruct((both, 2, rows, block, size), BF) for rows in ROWS],
+        scratch_shapes=[pltpu.VMEM((block, 2, groups, block, size), BF)],
+        cost_estimate=pl.CostEstimate(
+            flops=20 * block * size**3, bytes_accessed=8 * block * size**2, transcendentals=0
+        ),
+        name="screened",
+    )(place, swap, coulomb, *polar)
+
+
+def dyson_kernel(swap_ref, *refs):
+    sigmas, (free_ref, out_ref, whole) = refs[:CHUNKS], refs[CHUNKS:]
+    size = free_ref.shape[-1]
+    rest = sigmas[0].shape[0] // 2
+    step = pl.program_id(0)
+
+    @pl.when(step == 0)
+    def _():
+        gather_matrices(swap_ref, sigmas, whole, rest, lambda o: (o[0] * rest + o[2], o[1]))
+
+    for k in range(free_ref.shape[0]):
+        sigma = whole[step * free_ref.shape[0] + k].reshape(2 * size, size)
+        free = free_ref[k].reshape(2 * size, size)
+        both = dot(sigma, jnp.concatenate([free[:size], free[size:]], axis=1))
+        by_real, by_imag = both[:, :size], both[:, size:]
+        rr = (by_real[:size] - by_imag[size:]).astype(BF)
+        ri = (by_imag[:size] + by_real[size:]).astype(BF)
+        both = dot(free, jnp.concatenate([rr, ri], axis=1))
+        by_real, by_imag = both[:, :size], both[:, size:]
+        wide = free.astype(F32)
+        out_ref[k, 0] = (wide[:size] + by_real[:size] - by_imag[size:]).astype(BF)
+        out_ref[k, 1] = (wide[size:] + by_imag[:size] + by_real[size:]).astype(BF)
+
+
+def dyson(swap, sigma, free):
+    block, size = sigma[0].shape[-2:]
+    per = 2
+    energy_spec = pl.BlockSpec((per, 2, size, size), lambda e: (e, 0, 0, 0))
+    return pl.pallas_call(
+        dyson_kernel,
+        grid=(block // per,),
+        in_specs=[whole_spec(swap)] + [whole_spec(s) for s in sigma] + [energy_spec],
+        out_specs=energy_spec,
+        out_shape=jax.ShapeDtypeStruct(free.shape, BF),
+        scratch_shapes=[pltpu.VMEM((block, 2, size // block, block, size), BF)],
+        cost_estimate=pl.CostEstimate(
+            flops=18 * block * size**3, bytes_accessed=6 * free.size, transcendentals=0
+        ),
+        name="dyson",
+    )(swap, *sigma, free)
 
 
 def dft_tables(length, count):
@@ -66,23 +448,24 @@
     return jnp.einsum("eij,ejk->eik", left, right, preferred_element_type=jnp.float32)
 
 
-def per_device(g_lesser, g_greater, g_free, coulomb):
-    length = 2 * NE
-    upper, lower, backward = dft_tables(length, NE)
+def plain_device(ea, g_lesser, g_greater, g_free, coulomb):
+    ne = lax.axis_size(ea) * g_lesser.shape[0]
+    length = 2 * ne
+    upper, lower, backward = dft_tables(length, ne)
     tables = (upper, lower)
-    scale = 1.0 / (length * NE)
+    scale = 1.0 / (length * ne)
     greater_t = jnp.swapaxes(g_greater, 2, 3)
     lesser_rows, greater_rows = (
-        lax.all_to_all(g_lesser, "ea", split_axis=2, concat_axis=0, tiled=True),
-        lax.all_to_all(greater_t, "ea", split_axis=2, concat_axis=0, tiled=True),
+        lax.all_to_all(g_lesser, ea, split_axis=2, concat_axis=0, tiled=True),
+        lax.all_to_all(greater_t, ea, split_axis=2, concat_axis=0, tiled=True),
     )
     spec_lesser = forward(tables, lesser_rows, -1.0)
-    element_shape = (NE, lesser_rows.shape[2], lesser_rows.shape[3])
+    element_shape = (ne, lesser_rows.shape[2], lesser_rows.shape[3])
     spec_greater = forward(tables, greater_rows, 1.0)
     joined = complex_mul(spec_lesser, spec_greater)
     polar_real, polar_imag = inverse(backward, joined[0], joined[1], scale)
     polar_rows = restack(polar_real, polar_imag, element_shape)
-    polar = lax.all_to_all(polar_rows, "ea", split_axis=0, concat_axis=2, tiled=True)
+    polar = lax.all_to_all(polar_rows, ea, split_axis=0, concat_axis=2, tiled=True)
     mixed_real = jnp.einsum(
         "eij,jk->eik", polar[:, 0], coulomb, preferred_element_type=jnp.float32
     ).astype(jnp.bfloat16)
@@ -98,12 +481,12 @@
     )
     screen_imag = jnp.einsum("ij,ejk->eik", coulomb, inner_imag, preferred_element_type=jnp.float32)
     screen = jnp.stack([screen_real, screen_imag], axis=1).astype(jnp.bfloat16)
-    screen_rows = lax.all_to_all(screen, "ea", split_axis=2, concat_axis=0, tiled=True)
+    screen_rows = lax.all_to_all(screen, ea, split_axis=2, concat_axis=0, tiled=True)
     spec_screen = forward(tables, screen_rows, -1.0)
     folded = complex_mul(spec_lesser, spec_screen)
     sigma_real, sigma_imag = inverse(backward, folded[0], folded[1], scale)
     sigma_rows = restack(sigma_real, sigma_imag, element_shape)
-    sigma = lax.all_to_all(sigma_rows, "ea", split_axis=0, concat_axis=2, tiled=True)
+    sigma = lax.all_to_all(sigma_rows, ea, split_axis=0, concat_axis=2, tiled=True)
     free_real = g_free[:, 0]
     free_imag = g_free[:, 1]
     right_real = (batched(sigma[:, 0], free_real) - batched(sigma[:, 1], free_imag)).astype(
@@ -125,16 +508,79 @@
     return jnp.stack([out_real, out_imag], axis=1).astype(jnp.bfloat16)
 
 
+def cube_exchange(blocks):
+    return lax.all_to_all(blocks, ("bias", "low", "rest"), split_axis=0, concat_axis=0, tiled=True)
+
+
+def plane_exchange(blocks):
+    return lax.all_to_all(blocks, ("bias", "rest"), split_axis=0, concat_axis=0, tiled=True)
+
+
+def turn(blocks, step):
+    return lax.ppermute(blocks, ("half", "low"), [(i, i ^ step) for i in range(4)])
+
+
+def cube_device(g_lesser, g_greater, g_free, coulomb):
+    block = g_lesser.shape[0]
+    rest = lax.axis_size("rest")
+    half = lax.axis_index("half").astype(jnp.int32)
+    low = lax.axis_index("low").astype(jnp.int32)
+    place = jnp.stack([half, low])
+    spots = [(half ^ (s >> 1), low ^ (s & 1)) for s in range(4)]
+    swap = swap_matrix(block)
+    tables = spectral_tables(
+        4 * rest * block,
+        [2 * h + l for h, l in spots],
+        [(x * 2 + l) * rest + r for x in range(2) for r in range(rest) for l in range(2)],
+    )
+    polar, specs = [], []
+    for c in range(CHUNKS):
+        packed = pack(swap, g_lesser, g_greater, c)
+        own = plane_exchange(packed)
+        own = own.reshape((2, rest) + own.shape[1:])
+        blocks = [
+            lax.dynamic_slice(
+                own, (h, 0, l, 0, 0, 0, 0, 0), (1, rest, 1) + own.shape[3:]
+            ).reshape((rest,) + own.shape[3:])
+            for h, l in spots
+        ]
+        for s in (1, 2, 3):
+            blocks[s] = turn(blocks[s], s)
+        p, spec = polarization(tables, blocks)
+        polar.append(cube_exchange(p))
+        specs.append(spec)
+    screens = screened(place, swap, coulomb, polar)
+    sigma = []
+    for c in range(CHUNKS):
+        own, away = screens[c], screens[CHUNKS + c]
+        came = turn(away, 1)
+        own = lax.dynamic_update_slice(own, came[:, None], (0, 1 - low, 0, 0, 0, 0))
+        screen = plane_exchange(own)
+        own, *away = self_energy(place, tables, specs[c], screen)
+        for s in (1, 2, 3):
+            h, l = spots[s]
+            came = turn(away[s - 1], s)
+            came = came.reshape((1, rest, 1) + came.shape[1:])
+            own = lax.dynamic_update_slice(own, came, (h, 0, l, 0, 0, 0, 0))
+        sigma.append(plane_exchange(own.reshape((2 * rest,) + own.shape[2:])))
+    return dyson(swap, sigma, g_free)
+
+
 def solution(mesh):
+    bias, ea = mesh.shape["bias"], mesh.shape["ea"]
+    axes = ("bias", "ea")
+    cut = bias == 2 and ea % 4 == 0
+
+    def body(g_lesser, g_greater, g_free, coulomb):
+        block, _, size, _ = g_lesser.shape
+        if cut and block == 16 and size == block * ea:
+            return cube_device(g_lesser, g_greater, g_free, coulomb)
+        return plain_device(axes[1:], g_lesser, g_greater, g_free, coulomb)
+
+    if cut:
+        mesh = Mesh(mesh.devices.reshape(bias, 2, 2, ea // 4), ("bias", "half", "low", "rest"))
+        axes = ("bias", "half", "low", "rest")
+    spec = P(axes, None, None, None)
     return jax.shard_map(
-        per_device,
-        mesh=mesh,
-        in_specs=(
-            P(("bias", "ea"), None, None, None),
-            P(("bias", "ea"), None, None, None),
-            P(("bias", "ea"), None, None, None),
-            P(),
-        ),
-        out_specs=P(("bias", "ea"), None, None, None),
-        check_vma=False,
-    )
+        body, mesh=mesh, in_specs=(spec, spec, spec, P()), out_specs=spec, check_vma=False
+    )

time: 776 us -> 624 us (0.80)
  blocking collectives: 209 us -> 18.7 us
  matrix products: 179 us -> 0 us
  waiting for transfers between devices: 177 us -> 316 us
  Pallas kernels: 0 us -> 110 us
  other arithmetic: 103 us -> 11.7 us
  starting transfers between devices: 46.3 us -> 113 us
  local copies, waits for them, and re-layouts: 56.6 us -> 48.3 us
    ppermute x0 -> x28, waiting for transfers between devices: none -> 258 us  [turn(): lax.ppermute(blocks, ('half', 'low'), [(i, i ^ step) for i in range(4)])]
    all_to_all x2 -> x1, blocking collectives: 209 us -> 18.7 us  [plane_exchange(): lax.all_to_all(blocks, ('bias', 'rest'), split_axis=0, concat_axis=0, til...]
    dot_general x22 -> x0, matrix products: 179 us -> none  [the longest x3 74.7 us: forward(): result = result + jnp.dot(lower, joined, preferred_element_type=jnp.float32)]
    all_to_all x3 -> x15, waiting for transfers between devices: 177 us -> 58.2 us  [the longest x11 43.5 us: plane_exchange(): lax.all_to_all(blocks, ('bias', 'rest'), split_axis=0, concat_axis=0, til...]
    pallas_call x0 -> x14, Pallas kernels: none -> 110 us  [the longest x4 29.1 us: polarization(): pl.pallas_call(polar_kernel, in_specs=[VMEM] * 7, out_specs=[VMEM] * 2, o...]
    sub x2 -> x0, other arithmetic: 55.3 us -> none  [complex_mul(): left[0] * right[0] - left[1] * right[1]]
    ppermute x0 -> x28, starting transfers between devices: none -> 38 us  [turn(): lax.ppermute(blocks, ('half', 'low'), [(i, i ^ step) for i in range(4)])]
    all_to_all x3 -> x15, starting transfers between devices: 46.3 us -> 75.2 us  [the longest x11 55.6 us: plane_exchange(): lax.all_to_all(blocks, ('bias', 'rest'), split_axis=0, concat_axis=0, til...]
  transfers between devices with their start and end apart: 3 -> 43, of which waited for: 3 -> 20; matrix products, arithmetic and copies ran while one was open for 7% -> 8% of each run, Pallas kernels for 0% -> 11%
where the time goes in v2:
time: 624 us; the launch traced here: 619 us
  waiting for transfers between devices  316 us (51%)
  starting transfers between devices  113 us (18%)
  Pallas kernels  110 us (18%)
  local copies, waits for them, and re-layouts  48.3 us (8%)
  blocking collectives  18.7 us (3%)
  other arithmetic  11.7 us (2%)
    ppermute x28, waiting for transfers between devices, turn(): lax.ppermute(blocks, ('half', 'low'), [(i, i ^ step) for i in range(4)])  258 us
    all_to_all x11, starting transfers between devices, plane_exchange(): lax.all_to_all(blocks, ('bias', 'rest'), split_axis=0, concat_axis=0, til...  55.6 us
    all_to_all x11, waiting for transfers between devices, plane_exchange(): lax.all_to_all(blocks, ('bias', 'rest'), split_axis=0, concat_axis=0, til...  43.5 us
    ppermute x28, starting transfers between devices, turn(): lax.ppermute(blocks, ('half', 'low'), [(i, i ^ step) for i in range(4)])  38 us
    pallas_call x4, Pallas kernels, polarization(): pl.pallas_call(polar_kernel, in_specs=[VMEM] * 7, out_specs=[VMEM] * 2, o...  29.1 us
    pallas_call x4, Pallas kernels, self_energy(): pl.pallas_call(fold_kernel, in_specs=[SMEM] + [VMEM] * 4, out_specs=[VMEM...  27.1 us
    pallas_call x1, Pallas kernels, screened(): pl.pallas_call(screen_kernel, in_specs=[SMEM] + [VMEM] * (2 + CHUNKS), ou...  22.3 us
    unnamed x120, local copies, waits for them, and re-layouts  21.2 us
  transfers between devices with their start and end apart: 43, of which 20 were waited for; matrix products, arithmetic and copies ran while one was open for 8% of the time, Pallas kernels for 11%

profile of v2, /device:TPU:1, one launch (start us, length us, event | category | flops | bytes accessed | tf_op | source)
XLA Modules:
  0.0 618.5 jit_solution(1118923823447987827)
XLA Ops:
  5.9 5.4 all-to-all-start.6
  47.1 18.9 %all-to-all-done.2 = bf16[8,2,2,2,4,16,256]{6,5,4,3,2,1,0:T(8,128)(2,1)} async-done(((bf16[8,2,2,2,4,16,256]{6,5,4,3,2,1,0:T(8,128)(2,1)}), bf16[8,2,2,2,4,16,256]{6,5,4,3,2,1,0:T(8,128)(2,1)}, u32[]{:S(2)}, u32[]{:S(2)}) %all-to-all-start.2) | async-done | bytes 2097184 | tf_op jit(solution)/shard_map/all_to_all | solution.py:516
  75.5 20.7 %all-to-all-done.4 = bf16[8,2,2,2,4,16,256]{6,5,4,3,2,1,0:T(8,128)(2,1)} async-done(((bf16[8,2,2,2,4,16,256]{6,5,4,3,2,1,0:T(8,128)(2,1)}), bf16[8,2,2,2,4,16,256]{6,5,4,3,2,1,0:T(8,128)(2,1)}, u32[]{:S(2)}, u32[]{:S(2)}) %all-to-all-start.4) | async-done | bytes 2097184 | tf_op jit(solution)/shard_map/all_to_all | solution.py:516
  120.6 32.7 %collective-permute-done.10.refs_2_ = bf16[4,2,2,4,16,256]{5,4,3,2,1,0:T(8,128)(2,1)} collective-permute-done((bf16[4,2,2,4,16,256]{5,4,3,2,1,0:T(8,128)(2,1)}, bf16[4,2,2,4,16,256]{5,4,3,2,1,0:T(8,128)(2,1)}, u32[]{:S(2)}, u32[]{:S(2)}) %collective-permute-start.10) | collective-permute-done | bytes 524320 | tf_op jit(solution)/shard_map/ppermute | solution.py:520
  153.3 7.3 %polarization.7 = (bf16[16,2,4,16,256]{4,3,2,1,0:T(8,128)(2,1)}, bf16[2,1024,512]{2,1,0:T(8,128)(2,1)}) custom-call(bf16[1024,512]{1,0:T(8,128)(2,1)} %copy.11.minus_ref, bf16[1024,512]{1,0:T(8,128)(2,1)} %copy.12.plus_ref, bf16[512,1024]{1,0:T(8,128)(2,1)} %fusion.back_ref, bf16[4,2,2,4,16,256]{5,4,3,2,1,0:T(8,128)(2,1)} %get-tuple-element.94.refs_0_, ...), custom_call_target="tpu_custom_call" | custom-call | flops 3221225472 | bytes 5242880 | tf_op jit(solution)/shard_map/polarization/pallas_call | solution.py:191
  171.5 20.7 %collective-permute-done.5.refs_3_ = bf16[4,2,2,4,16,256]{5,4,3,2,1,0:T(8,128)(2,1)S(1)} collective-permute-done((bf16[4,2,2,4,16,256]{5,4,3,2,1,0:T(8,128)(2,1)S(1)}, bf16[4,2,2,4,16,256]{5,4,3,2,1,0:T(8,128)(2,1)S(1)}, u32[]{:S(2)}, u32[]{:S(2)}) %collective-permute-start.5) | collective-permute-done | bytes 524320 | tf_op jit(solution)/shard_map/ppermute | solution.py:520
  192.2 23.6 %collective-permute-done.4.refs_2_ = bf16[4,2,2,4,16,256]{5,4,3,2,1,0:T(8,128)(2,1)S(1)} collective-permute-done((bf16[4,2,2,4,16,256]{5,4,3,2,1,0:T(8,128)(2,1)S(1)}, bf16[4,2,2,4,16,256]{5,4,3,2,1,0:T(8,128)(2,1)S(1)}, u32[]{:S(2)}, u32[]{:S(2)}) %collective-permute-start.4) | collective-permute-done | bytes 524320 | tf_op jit(solution)/shard_map/ppermute | solution.py:520
  217.4 7.3 %polarization.5 = (bf16[16,2,4,16,256]{4,3,2,1,0:T(8,128)(2,1)}, bf16[2,1024,512]{2,1,0:T(8,128)(2,1)}) custom-call(bf16[1024,512]{1,0:T(8,128)(2,1)} %copy.11.minus_ref, bf16[1024,512]{1,0:T(8,128)(2,1)} %copy.12.plus_ref, bf16[512,1024]{1,0:T(8,128)(2,1)} %fusion.back_ref, bf16[4,2,2,4,16,256]{5,4,3,2,1,0:T(8,128)(2,1)} %get-tuple-element.102.refs_0_, ...), custom_call_target="tpu_custom_call" | custom-call | flops 3221225472 | bytes 5242880 | tf_op jit(solution)/shard_map/polarization/pallas_call | solution.py:191
  235.7 20.7 %collective-permute-done.8.refs_3_ = bf16[4,2,2,4,16,256]{5,4,3,2,1,0:T(8,128)(2,1)S(1)} collective-permute-done((bf16[4,2,2,4,16,256]{5,4,3,2,1,0:T(8,128)(2,1)S(1)}, bf16[4,2,2,4,16,256]{5,4,3,2,1,0:T(8,128)(2,1)S(1)}, u32[]{:S(2)}, u32[]{:S(2)}) %collective-permute-start.8) | collective-permute-done | bytes 524320 | tf_op jit(solution)/shard_map/ppermute | solution.py:520
  256.4 23.6 %collective-permute-done.7.refs_2_ = bf16[4,2,2,4,16,256]{5,4,3,2,1,0:T(8,128)(2,1)S(1)} collective-permute-done((bf16[4,2,2,4,16,256]{5,4,3,2,1,0:T(8,128)(2,1)S(1)}, bf16[4,2,2,4,16,256]{5,4,3,2,1,0:T(8,128)(2,1)S(1)}, u32[]{:S(2)}, u32[]{:S(2)}) %collective-permute-start.7) | collective-permute-done | bytes 524320 | tf_op jit(solution)/shard_map/ppermute | solution.py:520
  280.9 7.3 %polarization.6 = (bf16[16,2,4,16,256]{4,3,2,1,0:T(8,128)(2,1)}, bf16[2,1024,512]{2,1,0:T(8,128)(2,1)}) custom-call(bf16[1024,512]{1,0:T(8,128)(2,1)} %copy.11.minus_ref, bf16[1024,512]{1,0:T(8,128)(2,1)} %copy.12.plus_ref, bf16[512,1024]{1,0:T(8,128)(2,1)} %fusion.back_ref, bf16[4,2,2,4,16,256]{5,4,3,2,1,0:T(8,128)(2,1)} %get-tuple-element.98.refs_0_, ...), custom_call_target="tpu_custom_call" | custom-call | flops 3221225472 | bytes 5242880 | tf_op jit(solution)/shard_map/polarization/pallas_call | solution.py:191
  299.2 20.7 %collective-permute-done.2.refs_3_ = bf16[4,2,2,4,16,256]{5,4,3,2,1,0:T(8,128)(2,1)S(1)} collective-permute-done((bf16[4,2,2,4,16,256]{5,4,3,2,1,0:T(8,128)(2,1)S(1)}, bf16[4,2,2,4,16,256]{5,4,3,2,1,0:T(8,128)(2,1)S(1)}, u32[]{:S(2)}, u32[]{:S(2)}) %collective-permute-start.2) | collective-permute-done | bytes 524320 | tf_op jit(solution)/shard_map/ppermute | solution.py:520
  319.9 23.6 %collective-permute-done.1.refs_2_ = bf16[4,2,2,4,16,256]{5,4,3,2,1,0:T(8,128)(2,1)S(1)} collective-permute-done((bf16[4,2,2,4,16,256]{5,4,3,2,1,0:T(8,128)(2,1)S(1)}, bf16[4,2,2,4,16,256]{5,4,3,2,1,0:T(8,128)(2,1)S(1)}, u32[]{:S(2)}, u32[]{:S(2)}) %collective-permute-start.1) | collective-permute-done | bytes 524320 | tf_op jit(solution)/shard_map/ppermute | solution.py:520
  344.6 7.3 %polarization.4 = (bf16[16,2,4,16,256]{4,3,2,1,0:T(8,128)(2,1)}, bf16[2,1024,512]{2,1,0:T(8,128)(2,1)}) custom-call(bf16[1024,512]{1,0:T(8,128)(2,1)} %copy.11.minus_ref, bf16[1024,512]{1,0:T(8,128)(2,1)} %copy.12.plus_ref, bf16[512,1024]{1,0:T(8,128)(2,1)} %fusion.back_ref, bf16[4,2,2,4,16,256]{5,4,3,2,1,0:T(8,128)(2,1)} %get-tuple-element.106.refs_0_, ...), custom_call_target="tpu_custom_call" | custom-call | flops 3221225472 | bytes 5242880 | tf_op jit(solution)/shard_map/polarization/pallas_call | solution.py:191
  357.3 14.7 %all-to-all-done.1.refs_0_ = bf16[16,2,4,16,256]{4,3,2,1,0:T(8,128)(2,1)S(1)} async-done(((bf16[16,2,4,16,256]{4,3,2,1,0:T(8,128)(2,1)}), bf16[16,2,4,16,256]{4,3,2,1,0:T(8,128)(2,1)S(1)}, u32[]{:S(2)}, u32[]{:S(2)}) %all-to-all-start.1) | async-done | bytes 1048608 | tf_op jit(solution)/shard_map/all_to_all | solution.py:512
  373.0 22.3 %screened.1 = (bf16[8,2,2,4,16,256]{5,4,3,2,1,0:T(8,128)(2,1)}, bf16[8,2,2,4,16,256]{5,4,3,2,1,0:T(8,128)(2,1)}, bf16[8,2,2,4,16,256]{5,4,3,2,1,0:T(8,128)(2,1)}...) custom-call(s32[2]{0:T(128)} %pad_add_fusion.place_ref, ...), custom_call_target="tpu_custom_call" | custom-call | flops 5368709120 | bytes 8388608 | tf_op jit(solution)/shard_map/screened/pallas_call | solution.py:337
  395.3 12.7 %collective-permute-done.12 = bf16[8,2,4,16,256]{4,3,2,1,0:T(8,128)(2,1)S(1)} collective-permute-done((bf16[8,2,4,16,256]{4,3,2,1,0:T(8,128)(2,1)}, bf16[8,2,4,16,256]{4,3,2,1,0:T(8,128)(2,1)S(1)}, u32[]{:S(2)}, u32[]{:S(2)}) %collective-permute-start.12) | collective-permute-done | bytes 524320 | tf_op jit(solution)/shard_map/ppermute | solution.py:520
  409.0 5.3 all-to-all-start.8
  414.3 13.5 %collective-permute-done.16 = bf16[8,2,4,16,256]{4,3,2,1,0:T(8,128)(2,1)S(1)} collective-permute-done((bf16[8,2,4,16,256]{4,3,2,1,0:T(8,128)(2,1)}, bf16[8,2,4,16,256]{4,3,2,1,0:T(8,128)(2,1)S(1)}, u32[]{:S(2)}, u32[]{:S(2)}) %collective-permute-start.16) | collective-permute-done | bytes 524320 | tf_op jit(solution)/shard_map/ppermute | solution.py:520
  433.8 13.7 %collective-permute-done.20 = bf16[8,2,4,16,256]{4,3,2,1,0:T(8,128)(2,1)S(1)} collective-permute-done((bf16[8,2,4,16,256]{4,3,2,1,0:T(8,128)(2,1)}, bf16[8,2,4,16,256]{4,3,2,1,0:T(8,128)(2,1)S(1)}, u32[]{:S(2)}, u32[]{:S(2)}) %collective-permute-start.20) | collective-permute-done | bytes 524320 | tf_op jit(solution)/shard_map/ppermute | solution.py:520
  455.4 6.8 %self_energy.4 = (bf16[2,4,2,2,4,16,256]{6,5,4,3,2,1,0:T(8,128)(2,1)}, bf16[4,2,4,16,256]{4,3,2,1,0:T(8,128)(2,1)}, bf16[4,2,4,16,256]{4,3,2,1,0:T(8,128)(2,1)}, bf16[4,2,4,16,256]{4,3,2,1,0:T(8,128)(2,1)}) custom-call(s32[2]{0:T(128)} %pad_add_fusion.place_ref, bf16[1024,512]{1,0:T(8,128)(2,1)} %copy.31.minus_ref, ...), custom_call_target="tpu_custom_call" | custom-call | flops 2147483648 | bytes 4194304 | tf_op jit(solution)/shard_map/self_energy/pallas_call | solution.py:240
  468.6 5.5 all-to-all-start.14
  476.3 6.7 %self_energy.5 = (bf16[2,4,2,2,4,16,256]{6,5,4,3,2,1,0:T(8,128)(2,1)}, bf16[4,2,4,16,256]{4,3,2,1,0:T(8,128)(2,1)}, bf16[4,2,4,16,256]{4,3,2,1,0:T(8,128)(2,1)}, bf16[4,2,4,16,256]{4,3,2,1,0:T(8,128)(2,1)}) custom-call(s32[2]{0:T(128)} %pad_add_fusion.place_ref, bf16[1024,512]{1,0:T(8,128)(2,1)} %copy.31.minus_ref, ...), custom_call_target="tpu_custom_call" | custom-call | flops 2147483648 | bytes 4194304 | tf_op jit(solution)/shard_map/self_energy/pallas_call | solution.py:240
  484.2 10.3 %collective-permute-done.14 = bf16[4,2,4,16,256]{4,3,2,1,0:T(8,128)(2,1)S(1)} collective-permute-done((bf16[4,2,4,16,256]{4,3,2,1,0:T(8,128)(2,1)}, bf16[4,2,4,16,256]{4,3,2,1,0:T(8,128)(2,1)S(1)}, u32[]{:S(2)}, u32[]{:S(2)}) %collective-permute-start.14) | collective-permute-done | bytes 262176 | tf_op jit(solution)/shard_map/ppermute | solution.py:520
  500.3 6.1 collective-permute-start.18
  507.4 6.8 %self_energy.6 = (bf16[2,4,2,2,4,16,256]{6,5,4,3,2,1,0:T(8,128)(2,1)}, bf16[4,2,4,16,256]{4,3,2,1,0:T(8,128)(2,1)}, bf16[4,2,4,16,256]{4,3,2,1,0:T(8,128)(2,1)}, bf16[4,2,4,16,256]{4,3,2,1,0:T(8,128)(2,1)}) custom-call(s32[2]{0:T(128)} %pad_add_fusion.place_ref, bf16[1024,512]{1,0:T(8,128)(2,1)} %copy.31.minus_ref, ...), custom_call_target="tpu_custom_call" | custom-call | flops 2147483648 | bytes 4194304 | tf_op jit(solution)/shard_map/self_energy/pallas_call | solution.py:240
  515.0 9.5 %collective-permute-done.18 = bf16[4,2,4,16,256]{4,3,2,1,0:T(8,128)(2,1)S(1)} collective-permute-done((bf16[4,2,4,16,256]{4,3,2,1,0:T(8,128)(2,1)}, bf16[4,2,4,16,256]{4,3,2,1,0:T(8,128)(2,1)S(1)}, u32[]{:S(2)}, u32[]{:S(2)}) %collective-permute-start.18) | collective-permute-done | bytes 262176 | tf_op jit(solution)/shard_map/ppermute | solution.py:520
  537.6 6.8 %self_energy.7 = (bf16[2,4,2,2,4,16,256]{6,5,4,3,2,1,0:T(8,128)(2,1)}, bf16[4,2,4,16,256]{4,3,2,1,0:T(8,128)(2,1)}, bf16[4,2,4,16,256]{4,3,2,1,0:T(8,128)(2,1)}, bf16[4,2,4,16,256]{4,3,2,1,0:T(8,128)(2,1)}) custom-call(s32[2]{0:T(128)} %pad_add_fusion.place_ref, bf16[1024,512]{1,0:T(8,128)(2,1)} %copy.31.minus_ref, ...), custom_call_target="tpu_custom_call" | custom-call | flops 2147483648 | bytes 4194304 | tf_op jit(solution)/shard_map/self_energy/pallas_call | solution.py:240
  545.3 8.4 %collective-permute-done.22 = bf16[4,2,4,16,256]{4,3,2,1,0:T(8,128)(2,1)} collective-permute-done((bf16[4,2,4,16,256]{4,3,2,1,0:T(8,128)(2,1)}, bf16[4,2,4,16,256]{4,3,2,1,0:T(8,128)(2,1)}, u32[]{:S(2)}, u32[]{:S(2)}) %collective-permute-start.22) | collective-permute-done | bytes 262176 | tf_op jit(solution)/shard_map/ppermute | solution.py:520
  568.8 16.1 %collective-permute-done.26 = bf16[4,2,4,16,256]{4,3,2,1,0:T(8,128)(2,1)S(1)} collective-permute-done((bf16[4,2,4,16,256]{4,3,2,1,0:T(8,128)(2,1)}, bf16[4,2,4,16,256]{4,3,2,1,0:T(8,128)(2,1)S(1)}, u32[]{:S(2)}, u32[]{:S(2)}) %collective-permute-start.26) | collective-permute-done | bytes 262176 | tf_op jit(solution)/shard_map/ppermute | solution.py:520
  584.9 18.7 %all_to_all.80.refs_3_ = bf16[8,2,2,4,16,256]{5,4,3,2,1,0:T(8,128)(2,1)} all-to-all(bf16[8,2,2,4,16,256]{5,4,3,2,1,0:T(8,128)(2,1)S(1)} %bitcast.135), channel_id=1, replica_groups=mesh['bias'=2,'half'=2,'low'=2,'rest'=4] {'bias','rest'}, dimensions={0} | all-to-all | bytes 2097152 | tf_op jit(solution)/shard_map/all_to_all | solution.py:516
  603.6 14.9 %dyson.1 = bf16[16,2,256,256]{3,2,1,0:T(8,128)(2,1)} custom-call(bf16[256,256]{1,0:T(8,128)(2,1)} %fusion.1.swap_ref, bf16[8,2,2,4,16,256]{5,4,3,2,1,0:T(8,128)(2,1)} %copy-done.5, bf16[8,2,2,4,16,256]{5,4,3,2,1,0:T(8,128)(2,1)} %copy-done.9, bf16[8,2,2,4,16,256]{5,4,3,2,1,0:T(8,128)(2,1)} %copy-done.14, bf16[8,2,2,4,16,256]{5,4,3,2,1,0:T(8,128)(2,1)} %all_to_all.80.refs_3_, ...), custom_call_target="tpu_custom_call" | custom-call | flops 4831838208 | bytes 12582912 | tf_op jit(solution)/shard_map/dyson/pallas_call | solution.py:379
  (232 shorter events, 179.6 us)
Async XLA Ops:
  5.9 30.1 %all-to-all-start.6 = ((bf16[8,2,2,2,4,16,256]{6,5,4,3,2,1,0:T(8,128)(2,1)}), bf16[8,2,2,2,4,16,256]{6,5,4,3,2,1,0:T(8,128)(2,1)S(1)}, u32[]{:S(2)}, u32[]{:S(2)}) async-start(bf16[8,2,2,2,4,16,256]{6,5,4,3,2,1,0:T(8,128)(2,1)} %pack.7), calls=%async_computation.6 | async-start | bytes 4194304 | tf_op jit(solution)/shard_map/all_to_all | solution.py:516
  36.0 30.1 %all-to-all-start.2 = ((bf16[8,2,2,2,4,16,256]{6,5,4,3,2,1,0:T(8,128)(2,1)}), bf16[8,2,2,2,4,16,256]{6,5,4,3,2,1,0:T(8,128)(2,1)}, u32[]{:S(2)}, u32[]{:S(2)}) async-start(bf16[8,2,2,2,4,16,256]{6,5,4,3,2,1,0:T(8,128)(2,1)} %pack.5), calls=%async_computation.2 | async-start | bytes 4194304 | tf_op jit(solution)/shard_map/all_to_all | solution.py:516
  66.1 30.1 %all-to-all-start.4 = ((bf16[8,2,2,2,4,16,256]{6,5,4,3,2,1,0:T(8,128)(2,1)}), bf16[8,2,2,2,4,16,256]{6,5,4,3,2,1,0:T(8,128)(2,1)}, u32[]{:S(2)}, u32[]{:S(2)}) async-start(bf16[8,2,2,2,4,16,256]{6,5,4,3,2,1,0:T(8,128)(2,1)} %pack.6), calls=%async_computation.4 | async-start | bytes 4194304 | tf_op jit(solution)/shard_map/all_to_all | solution.py:516
  96.1 64.5 %all-to-all-start = ((bf16[8,2,2,2,4,16,256]{6,5,4,3,2,1,0:T(8,128)(2,1)}), bf16[8,2,2,2,4,16,256]{6,5,4,3,2,1,0:T(8,128)(2,1)}, u32[]{:S(2)}, u32[]{:S(2)}) async-start(bf16[8,2,2,2,4,16,256]{6,5,4,3,2,1,0:T(8,128)(2,1)} %pack.4), calls=%async_computation | async-start | bytes 4194304 | tf_op jit(solution)/shard_map/all_to_all | solution.py:516
  108.3 45.0 %collective-permute-start.10 = (bf16[4,2,2,4,16,256]{5,4,3,2,1,0:T(8,128)(2,1)}, bf16[4,2,2,4,16,256]{5,4,3,2,1,0:T(8,128)(2,1)}, u32[]{:S(2)}, u32[]{:S(2)}) collective-permute-start(bf16[4,2,2,4,16,256]{5,4,3,2,1,0:T(8,128)(2,1)} %get-tuple-element.92), channel_id=1, source_target_pairs={{0,8},{4,12},{8,0},{12,4},{1,9},{5,13},{9,1},{13,5},{2,10},{6,14},... | collective-permute-start | bytes 1572872 | tf_op jit(solution)/shard_map/ppermute | solution.py:520
  108.3 45.0 %collective-permute-start.9 = (bf16[4,2,2,4,16,256]{5,4,3,2,1,0:T(8,128)(2,1)}, bf16[4,2,2,4,16,256]{5,4,3,2,1,0:T(8,128)(2,1)}, u32[]{:S(2)}, u32[]{:S(2)}) collective-permute-start(bf16[4,2,2,4,16,256]{5,4,3,2,1,0:T(8,128)(2,1)} %get-tuple-element.93), channel_id=1, source_target_pairs={{0,4},{4,0},{8,12},{12,8},{1,5},{5,1},{9,13},{13,9},{2,6},{6,2},{1... | collective-permute-start | bytes 1572872 | tf_op jit(solution)/shard_map/ppermute | solution.py:520
  160.6 64.1 %all-to-all-start.7 = ((bf16[16,2,4,16,256]{4,3,2,1,0:T(8,128)(2,1)}), bf16[16,2,4,16,256]{4,3,2,1,0:T(8,128)(2,1)S(1)}, u32[]{:S(2)}, u32[]{:S(2)}) async-start(bf16[16,2,4,16,256]{4,3,2,1,0:T(8,128)(2,1)} %get-tuple-element.55), calls=%async_computation.7 | async-start | bytes 2097152 | tf_op jit(solution)/shard_map/all_to_all | solution.py:512
  168.0 24.2 %collective-permute-start.5 = (bf16[4,2,2,4,16,256]{5,4,3,2,1,0:T(8,128)(2,1)S(1)}, bf16[4,2,2,4,16,256]{5,4,3,2,1,0:T(8,128)(2,1)S(1)}, u32[]{:S(2)}, u32[]{:S(2)}) collective-permute-start(bf16[4,2,2,4,16,256]{5,4,3,2,1,0:T(8,128)(2,1)S(1)} %get-tuple-element.99), channel_id=1, source_target_pairs={{0,12},{4,8},{8,4},{12,0},{1,13},{5,9},{9,5},{13,1},{2,14},{6,10},... | collective-permute-start | bytes 1572872 | tf_op jit(solution)/shard_map/ppermute | solution.py:520
  171.2 44.6 %collective-permute-start.4 = (bf16[4,2,2,4,16,256]{5,4,3,2,1,0:T(8,128)(2,1)S(1)}, bf16[4,2,2,4,16,256]{5,4,3,2,1,0:T(8,128)(2,1)S(1)}, u32[]{:S(2)}, u32[]{:S(2)}) collective-permute-start(bf16[4,2,2,4,16,256]{5,4,3,2,1,0:T(8,128)(2,1)S(1)} %get-tuple-element.100), channel_id=1, source_target_pairs={{0,8},{4,12},{8,0},{12,4},{1,9},{5,13},{9,1},{13,5},{2,10},{6,14},... | collective-permute-start | bytes 1572872 | tf_op jit(solution)/shard_map/ppermute | solution.py:520
  171.2 44.6 %collective-permute-start.3 = (bf16[4,2,2,4,16,256]{5,4,3,2,1,0:T(8,128)(2,1)S(1)}, bf16[4,2,2,4,16,256]{5,4,3,2,1,0:T(8,128)(2,1)S(1)}, u32[]{:S(2)}, u32[]{:S(2)}) collective-permute-start(bf16[4,2,2,4,16,256]{5,4,3,2,1,0:T(8,128)(2,1)S(1)} %get-tuple-element.101), channel_id=1, source_target_pairs={{0,4},{4,0},{8,12},{12,8},{1,5},{5,1},{9,13},{13,9},{2,6},{6,2},{1... | collective-permute-start | bytes 1572872 | tf_op jit(solution)/shard_map/ppermute | solution.py:520
  224.7 63.6 %all-to-all-start.3 = ((bf16[16,2,4,16,256]{4,3,2,1,0:T(8,128)(2,1)}), bf16[16,2,4,16,256]{4,3,2,1,0:T(8,128)(2,1)S(1)}, u32[]{:S(2)}, u32[]{:S(2)}) async-start(bf16[16,2,4,16,256]{4,3,2,1,0:T(8,128)(2,1)} %get-tuple-element.53), calls=%async_computation.3 | async-start | bytes 2097152 | tf_op jit(solution)/shard_map/all_to_all | solution.py:512
  232.1 24.2 %collective-permute-start.8 = (bf16[4,2,2,4,16,256]{5,4,3,2,1,0:T(8,128)(2,1)S(1)}, bf16[4,2,2,4,16,256]{5,4,3,2,1,0:T(8,128)(2,1)S(1)}, u32[]{:S(2)}, u32[]{:S(2)}) collective-permute-start(bf16[4,2,2,4,16,256]{5,4,3,2,1,0:T(8,128)(2,1)S(1)} %get-tuple-element.95), channel_id=1, source_target_pairs={{0,12},{4,8},{8,4},{12,0},{1,13},{5,9},{9,5},{13,1},{2,14},{6,10},... | collective-permute-start | bytes 1572872 | tf_op jit(solution)/shard_map/ppermute | solution.py:520
  235.4 44.6 %collective-permute-start.7 = (bf16[4,2,2,4,16,256]{5,4,3,2,1,0:T(8,128)(2,1)S(1)}, bf16[4,2,2,4,16,256]{5,4,3,2,1,0:T(8,128)(2,1)S(1)}, u32[]{:S(2)}, u32[]{:S(2)}) collective-permute-start(bf16[4,2,2,4,16,256]{5,4,3,2,1,0:T(8,128)(2,1)S(1)} %get-tuple-element.96), channel_id=1, source_target_pairs={{0,8},{4,12},{8,0},{12,4},{1,9},{5,13},{9,1},{13,5},{2,10},{6,14},... | collective-permute-start | bytes 1572872 | tf_op jit(solution)/shard_map/ppermute | solution.py:520
  235.4 44.6 %collective-permute-start.6 = (bf16[4,2,2,4,16,256]{5,4,3,2,1,0:T(8,128)(2,1)S(1)}, bf16[4,2,2,4,16,256]{5,4,3,2,1,0:T(8,128)(2,1)S(1)}, u32[]{:S(2)}, u32[]{:S(2)}) collective-permute-start(bf16[4,2,2,4,16,256]{5,4,3,2,1,0:T(8,128)(2,1)S(1)} %get-tuple-element.97), channel_id=1, source_target_pairs={{0,4},{4,0},{8,12},{12,8},{1,5},{5,1},{9,13},{13,9},{2,6},{6,2},{1... | collective-permute-start | bytes 1572872 | tf_op jit(solution)/shard_map/ppermute | solution.py:520
  288.3 63.6 %all-to-all-start.5 = ((bf16[16,2,4,16,256]{4,3,2,1,0:T(8,128)(2,1)}), bf16[16,2,4,16,256]{4,3,2,1,0:T(8,128)(2,1)S(1)}, u32[]{:S(2)}, u32[]{:S(2)}) async-start(bf16[16,2,4,16,256]{4,3,2,1,0:T(8,128)(2,1)} %get-tuple-element.54), calls=%async_computation.5 | async-start | bytes 2097152 | tf_op jit(solution)/shard_map/all_to_all | solution.py:512
  295.6 24.2 %collective-permute-start.2 = (bf16[4,2,2,4,16,256]{5,4,3,2,1,0:T(8,128)(2,1)S(1)}, bf16[4,2,2,4,16,256]{5,4,3,2,1,0:T(8,128)(2,1)S(1)}, u32[]{:S(2)}, u32[]{:S(2)}) collective-permute-start(bf16[4,2,2,4,16,256]{5,4,3,2,1,0:T(8,128)(2,1)S(1)} %get-tuple-element.103), channel_id=1, source_target_pairs={{0,12},{4,8},{8,4},{12,0},{1,13},{5,9},{9,5},{13,1},{2,14},{6,10},... | collective-permute-start | bytes 1572872 | tf_op jit(solution)/shard_map/ppermute | solution.py:520
  298.9 44.6 %collective-permute-start.1 = (bf16[4,2,2,4,16,256]{5,4,3,2,1,0:T(8,128)(2,1)S(1)}, bf16[4,2,2,4,16,256]{5,4,3,2,1,0:T(8,128)(2,1)S(1)}, u32[]{:S(2)}, u32[]{:S(2)}) collective-permute-start(bf16[4,2,2,4,16,256]{5,4,3,2,1,0:T(8,128)(2,1)S(1)} %get-tuple-element.104), channel_id=1, source_target_pairs={{0,8},{4,12},{8,0},{12,4},{1,9},{5,13},{9,1},{13,5},{2,10},{6,14},... | collective-permute-start | bytes 1572872 | tf_op jit(solution)/shard_map/ppermute | solution.py:520
  298.9 44.6 %collective-permute-start = (bf16[4,2,2,4,16,256]{5,4,3,2,1,0:T(8,128)(2,1)S(1)}, bf16[4,2,2,4,16,256]{5,4,3,2,1,0:T(8,128)(2,1)S(1)}, u32[]{:S(2)}, u32[]{:S(2)}) collective-permute-start(bf16[4,2,2,4,16,256]{5,4,3,2,1,0:T(8,128)(2,1)S(1)} %get-tuple-element.105), channel_id=1, source_target_pairs={{0,4},{4,0},{8,12},{12,8},{1,5},{5,1},{9,13},{13,9},{2,6},{6,2},{1... | collective-permute-start | bytes 1572872 | tf_op jit(solution)/shard_map/ppermute | solution.py:520
  351.8 20.2 %all-to-all-start.1 = ((bf16[16,2,4,16,256]{4,3,2,1,0:T(8,128)(2,1)}), bf16[16,2,4,16,256]{4,3,2,1,0:T(8,128)(2,1)S(1)}, u32[]{:S(2)}, u32[]{:S(2)}) async-start(bf16[16,2,4,16,256]{4,3,2,1,0:T(8,128)(2,1)} %get-tuple-element.52), calls=%async_computation.1 | async-start | bytes 2097152 | tf_op jit(solution)/shard_map/all_to_all | solution.py:512
  409.0 19.9 %all-to-all-start.8 = ((bf16[8,2,2,4,16,256]{5,4,3,2,1,0:T(8,128)(2,1)}), bf16[8,2,2,4,16,256]{5,4,3,2,1,0:T(8,128)(2,1)S(1)}, u32[]{:S(2)}, u32[]{:S(2)}) async-start(bf16[8,2,2,4,16,256]{5,4,3,2,1,0:T(8,128)(2,1)} %bitcast_dynamic-update-slice_fusion.3), calls=%async_computation.8 | async-start | bytes 2097152 | tf_op jit(solution)/shard_map/all_to_all | solution.py:516
  462.2 21.3 %collective-permute-start.13 = (bf16[4,2,4,16,256]{4,3,2,1,0:T(8,128)(2,1)}, bf16[4,2,4,16,256]{4,3,2,1,0:T(8,128)(2,1)S(1)}, u32[]{:S(2)}, u32[]{:S(2)}) collective-permute-start(bf16[4,2,4,16,256]{4,3,2,1,0:T(8,128)(2,1)} %get-tuple-element.59), channel_id=1, source_target_pairs={{0,4},{4,0},{8,12},{12,8},{1,5},{5,1},{9,13},{13,9},{2,6},{6,2},{1... | collective-permute-start | bytes 786440 | tf_op jit(solution)/shard_map/ppermute | solution.py:520
  468.6 27.4 %all-to-all-start.14 = ((bf16[8,2,2,4,16,256]{5,4,3,2,1,0:T(8,128)(2,1)}), bf16[8,2,2,4,16,256]{5,4,3,2,1,0:T(8,128)(2,1)S(1)}, u32[]{:S(2)}, u32[]{:S(2)}) async-start(bf16[8,2,2,4,16,256]{5,4,3,2,1,0:T(8,128)(2,1)} %bitcast_dynamic-update-slice_fusion), calls=%async_computation.14 | async-start | bytes 2097152 | tf_op jit(solution)/shard_map/all_to_all | solution.py:516
  474.1 20.4 %collective-permute-start.14 = (bf16[4,2,4,16,256]{4,3,2,1,0:T(8,128)(2,1)}, bf16[4,2,4,16,256]{4,3,2,1,0:T(8,128)(2,1)S(1)}, u32[]{:S(2)}, u32[]{:S(2)}) collective-permute-start(bf16[4,2,4,16,256]{4,3,2,1,0:T(8,128)(2,1)} %get-tuple-element.60), channel_id=1, source_target_pairs={{0,8},{4,12},{8,0},{12,4},{1,9},{5,13},{9,1},{13,5},{2,10},{6,14},... | collective-permute-start | bytes 786440 | tf_op jit(solution)/shard_map/ppermute | solution.py:520
  483.0 31.2 %collective-permute-start.17 = (bf16[4,2,4,16,256]{4,3,2,1,0:T(8,128)(2,1)}, bf16[4,2,4,16,256]{4,3,2,1,0:T(8,128)(2,1)S(1)}, u32[]{:S(2)}, u32[]{:S(2)}) collective-permute-start(bf16[4,2,4,16,256]{4,3,2,1,0:T(8,128)(2,1)} %get-tuple-element.66), channel_id=1, source_target_pairs={{0,4},{4,0},{8,12},{12,8},{1,5},{5,1},{9,13},{13,9},{2,6},{6,2},{1... | collective-permute-start | bytes 786440 | tf_op jit(solution)/shard_map/ppermute | solution.py:520
  496.0 30.0 %all-to-all-start.9 = ((bf16[8,2,2,4,16,256]{5,4,3,2,1,0:T(8,128)(2,1)}), bf16[8,2,2,4,16,256]{5,4,3,2,1,0:T(8,128)(2,1)S(1)}, u32[]{:S(2)}, u32[]{:S(2)}) async-start(bf16[8,2,2,4,16,256]{5,4,3,2,1,0:T(8,128)(2,1)} %bitcast.31), calls=%async_computation.9 | async-start | bytes 2097152 | tf_op jit(solution)/shard_map/all_to_all | solution.py:516
  500.3 24.2 %collective-permute-start.18 = (bf16[4,2,4,16,256]{4,3,2,1,0:T(8,128)(2,1)}, bf16[4,2,4,16,256]{4,3,2,1,0:T(8,128)(2,1)S(1)}, u32[]{:S(2)}, u32[]{:S(2)}) collective-permute-start(bf16[4,2,4,16,256]{4,3,2,1,0:T(8,128)(2,1)} %get-tuple-element.67), channel_id=1, source_target_pairs={{0,8},{4,12},{8,0},{12,4},{1,9},{5,13},{9,1},{13,5},{2,10},{6,14},... | collective-permute-start | bytes 786440 | tf_op jit(solution)/shard_map/ppermute | solution.py:520
  514.3 30.2 %collective-permute-start.21 = (bf16[4,2,4,16,256]{4,3,2,1,0:T(8,128)(2,1)}, bf16[4,2,4,16,256]{4,3,2,1,0:T(8,128)(2,1)S(1)}, u32[]{:S(2)}, u32[]{:S(2)}) collective-permute-start(bf16[4,2,4,16,256]{4,3,2,1,0:T(8,128)(2,1)} %get-tuple-element.73), channel_id=1, source_target_pairs={{0,4},{4,0},{8,12},{12,8},{1,5},{5,1},{9,13},{13,9},{2,6},{6,2},{1... | collective-permute-start | bytes 786440 | tf_op jit(solution)/shard_map/ppermute | solution.py:520
  526.0 31.0 %all-to-all-start.11 = ((bf16[8,2,2,4,16,256]{5,4,3,2,1,0:T(8,128)(2,1)}), bf16[8,2,2,4,16,256]{5,4,3,2,1,0:T(8,128)(2,1)S(1)}, u32[]{:S(2)}, u32[]{:S(2)}) async-start(bf16[8,2,2,4,16,256]{5,4,3,2,1,0:T(8,128)(2,1)} %bitcast.39), calls=%async_computation.11 | async-start | bytes 2097152 | tf_op jit(solution)/shard_map/all_to_all | solution.py:516
  531.0 22.7 %collective-permute-start.22 = (bf16[4,2,4,16,256]{4,3,2,1,0:T(8,128)(2,1)}, bf16[4,2,4,16,256]{4,3,2,1,0:T(8,128)(2,1)}, u32[]{:S(2)}, u32[]{:S(2)}) collective-permute-start(bf16[4,2,4,16,256]{4,3,2,1,0:T(8,128)(2,1)} %get-tuple-element.74), channel_id=1, source_target_pairs={{0,8},{4,12},{8,0},{12,4},{1,9},{5,13},{9,1},{13,5},{2,10},{6,14},... | collective-permute-start | bytes 786440 | tf_op jit(solution)/shard_map/ppermute | solution.py:520
  544.4 23.3 %collective-permute-start.25 = (bf16[4,2,4,16,256]{4,3,2,1,0:T(8,128)(2,1)}, bf16[4,2,4,16,256]{4,3,2,1,0:T(8,128)(2,1)}, u32[]{:S(2)}, u32[]{:S(2)}) collective-permute-start(bf16[4,2,4,16,256]{4,3,2,1,0:T(8,128)(2,1)} %get-tuple-element.80), channel_id=1, source_target_pairs={{0,4},{4,0},{8,12},{12,8},{1,5},{5,1},{9,13},{13,9},{2,6},{6,2},{1... | collective-permute-start | bytes 786440 | tf_op jit(solution)/shard_map/ppermute | solution.py:520
  557.0 27.9 %all-to-all-start.13 = ((bf16[8,2,2,4,16,256]{5,4,3,2,1,0:T(8,128)(2,1)}), bf16[8,2,2,4,16,256]{5,4,3,2,1,0:T(8,128)(2,1)S(1)}, u32[]{:S(2)}, u32[]{:S(2)}) async-start(bf16[8,2,2,4,16,256]{5,4,3,2,1,0:T(8,128)(2,1)} %bitcast.47), calls=%async_computation.13 | async-start | bytes 2097152 | tf_op jit(solution)/shard_map/all_to_all | solution.py:516
  562.0 22.8 %collective-permute-start.26 = (bf16[4,2,4,16,256]{4,3,2,1,0:T(8,128)(2,1)}, bf16[4,2,4,16,256]{4,3,2,1,0:T(8,128)(2,1)S(1)}, u32[]{:S(2)}, u32[]{:S(2)}) collective-permute-start(bf16[4,2,4,16,256]{4,3,2,1,0:T(8,128)(2,1)} %get-tuple-element.81), channel_id=1, source_target_pairs={{0,8},{4,12},{8,0},{12,4},{1,9},{5,13},{9,1},{13,5},{2,10},{6,14},... | collective-permute-start | bytes 786440 | tf_op jit(solution)/shard_map/ppermute | solution.py:520
  (45 other events, 605.1 us)

commit v3 on v2

--- a/solution.py
+++ b/solution.py
@@ -1,3 +1,4 @@
+import functools
 import math
 
 import jax
@@ -276,34 +277,70 @@
             body(tile, tile_owners(rows, rest, block, tile))
 
 
-def gather_matrices(swap_ref, refs, whole, rest, order):
+def gather_chunk(swap_ref, ref, whole, rest, order):
     block, size = whole.shape[-2:]
 
-    for ref, start in zip(refs, STARTS):
-
-        def body(tile, owners, ref=ref, start=start):
-            pieces = [
-                jnp.concatenate([ref[(*order(o), r)].reshape(-1, size) for o in owners], axis=0)
-                for r in range(2)
-            ]
-            to_matrices(swap_ref, whole, start + tile, pieces)
-
-        each_tile(ref.shape[-3], rest, block, body)
+    def body(tile, owners):
+        pieces = [
+            jnp.concatenate([ref[(*order(o), r)].reshape(-1, size) for o in owners], axis=0)
+            for r in range(2)
+        ]
+        to_matrices(swap_ref, whole, tile, pieces)
+
+    each_tile(ref.shape[-3], rest, block, body)
+
+
+def polar_order(rest):
+    return lambda o: ((o[0] * 2 + o[1]) * rest + o[2],)
+
+
+def sigma_order(rest):
+    return lambda o: (o[0] * rest + o[2], o[1])
+
+
+def chunk_shape(blocks):
+    rows, block, size = blocks.shape[-3:]
+    return (block, 2, rows, block, size)
+
+
+def gather_kernel(order, rest, swap_ref, ref, out_ref):
+    gather_chunk(swap_ref, ref, out_ref, rest, order)
+
+
+def gathered(swap, blocks, order, rest):
+    return pl.pallas_call(
+        functools.partial(gather_kernel, order, rest),
+        in_specs=[VMEM] * 2,
+        out_specs=VMEM,
+        out_shape=jax.ShapeDtypeStruct(chunk_shape(blocks), BF),
+        cost_estimate=pl.CostEstimate(
+            flops=2 * blocks.size * swap.shape[0],
+            bytes_accessed=4 * blocks.size,
+            transcendentals=0,
+        ),
+        name="gathered",
+    )(swap, blocks)
+
+
+def stacked_rows(refs, e):
+    size = refs[0].shape[-1]
+    return jnp.concatenate([ref[e, r].reshape(-1, size) for r in range(2) for ref in refs], axis=0)
 
 
 def screen_kernel(place_ref, swap_ref, coulomb_ref, *refs):
     ins, owns, aways = refs[:CHUNKS], refs[CHUNKS : 2 * CHUNKS], refs[2 * CHUNKS : 3 * CHUNKS]
-    whole = refs[-1]
+    last, whole = refs[3 * CHUNKS :]
     size = coulomb_ref.shape[0]
     block = whole.shape[-2]
-    rest = ins[0].shape[0] // 4
+    rest = ins[-1].shape[0] // 4
     low = place_ref[1]
-    gather_matrices(swap_ref, ins, whole, rest, lambda o: ((o[0] * 2 + o[1]) * rest + o[2],))
+    gather_chunk(swap_ref, ins[-1], last, rest, polar_order(rest))
+    parts = [*ins[:-1], last]
     volts = coulomb_ref[...]
 
     @pl.loop(0, block, unroll=2)
     def _(w):
-        mixed = dot(whole[w].reshape(2 * size, size), volts).astype(BF)
+        mixed = dot(stacked_rows(parts, w), volts).astype(BF)
         both = dot(mixed, jnp.concatenate([mixed[:size], mixed[size:]], axis=1))
         by_real, by_imag = both[:, :size], both[:, size:]
         nr = (mixed[:size].astype(F32) + (by_real[:size] - by_imag[size:])).astype(BF)
@@ -332,7 +369,7 @@
 
 
 def screened(place, swap, coulomb, polar):
-    groups, _, _, block, size = polar[0].shape
+    groups, _, _, block, size = polar[-1].shape
     both = groups // 2
     return pl.pallas_call(
         screen_kernel,
@@ -340,7 +377,10 @@
         out_specs=[VMEM] * (2 * CHUNKS),
         out_shape=[jax.ShapeDtypeStruct((both, 2, 2, rows, block, size), BF) for rows in ROWS]
         + [jax.ShapeDtypeStruct((both, 2, rows, block, size), BF) for rows in ROWS],
-        scratch_shapes=[pltpu.VMEM((block, 2, groups, block, size), BF)],
+        scratch_shapes=[
+            pltpu.VMEM(chunk_shape(polar[-1]), BF),
+            pltpu.VMEM((block, 2, groups, block, size), BF),
+        ],
         cost_estimate=pl.CostEstimate(
             flops=20 * block * size**3, bytes_accessed=8 * block * size**2, transcendentals=0
         ),
@@ -349,17 +389,18 @@
 
 
 def dyson_kernel(swap_ref, *refs):
-    sigmas, (free_ref, out_ref, whole) = refs[:CHUNKS], refs[CHUNKS:]
+    sigmas, (free_ref, out_ref, last) = refs[:CHUNKS], refs[CHUNKS:]
     size = free_ref.shape[-1]
-    rest = sigmas[0].shape[0] // 2
+    rest = sigmas[-1].shape[0] // 2
     step = pl.program_id(0)
 
     @pl.when(step == 0)
     def _():
-        gather_matrices(swap_ref, sigmas, whole, rest, lambda o: (o[0] * rest + o[2], o[1]))
-
+        gather_chunk(swap_ref, sigmas[-1], last, rest, sigma_order(rest))
+
+    parts = [*sigmas[:-1], last]
     for k in range(free_ref.shape[0]):
-        sigma = whole[step * free_ref.shape[0] + k].reshape(2 * size, size)
+        sigma = stacked_rows(parts, step * free_ref.shape[0] + k)
         free = free_ref[k].reshape(2 * size, size)
         both = dot(sigma, jnp.concatenate([free[:size], free[size:]], axis=1))
         by_real, by_imag = both[:, :size], both[:, size:]
@@ -373,16 +414,16 @@
 
 
 def dyson(swap, sigma, free):
-    block, size = sigma[0].shape[-2:]
+    block, size = sigma[-1].shape[-2:]
     per = 2
     energy_spec = pl.BlockSpec((per, 2, size, size), lambda e: (e, 0, 0, 0))
     return pl.pallas_call(
         dyson_kernel,
         grid=(block // per,),
-        in_specs=[whole_spec(swap)] + [whole_spec(s) for s in sigma] + [energy_spec],
+        in_specs=[VMEM] * (1 + len(sigma)) + [energy_spec],
         out_specs=energy_spec,
         out_shape=jax.ShapeDtypeStruct(free.shape, BF),
-        scratch_shapes=[pltpu.VMEM((block, 2, size // block, block, size), BF)],
+        scratch_shapes=[pltpu.VMEM(chunk_shape(sigma[-1]), BF)],
         cost_estimate=pl.CostEstimate(
             flops=18 * block * size**3, bytes_accessed=6 * free.size, transcendentals=0
         ),
@@ -547,7 +588,10 @@
         for s in (1, 2, 3):
             blocks[s] = turn(blocks[s], s)
         p, spec = polarization(tables, blocks)
-        polar.append(cube_exchange(p))
+        came = cube_exchange(p)
+        if c < CHUNKS - 1:
+            came = gathered(swap, came, polar_order(rest), rest)
+        polar.append(came)
         specs.append(spec)
     screens = screened(place, swap, coulomb, polar)
     sigma = []
@@ -562,7 +606,10 @@
             came = turn(away[s - 1], s)
             came = came.reshape((1, rest, 1) + came.shape[1:])
             own = lax.dynamic_update_slice(own, came, (h, 0, l, 0, 0, 0, 0))
-        sigma.append(plane_exchange(own.reshape((2 * rest,) + own.shape[2:])))
+        came = plane_exchange(own.reshape((2 * rest,) + own.shape[2:]))
+        if c < CHUNKS - 1:
+            came = gathered(swap, came, sigma_order(rest), rest)
+        sigma.append(came)
     return dyson(swap, sigma, g_free)
 
 

time: 624 us -> 624 us (level)
  blocking collectives: 18.7 us -> 0 us
  Pallas kernels: 110 us -> 124 us
  waiting for transfers between devices: 316 us -> 303 us
  local copies, waits for them, and re-layouts: 48.3 us -> 59.9 us
    all_to_all x1 -> x0, blocking collectives: 18.7 us -> none  [plane_exchange(): lax.all_to_all(blocks, ('bias', 'rest'), split_axis=0, concat_axis=0, til...]
    pallas_call x1 -> x7, Pallas kernels: 14.9 us -> 30.5 us  [the longest x6 17.4 us: gathered(): pl.pallas_call(functools.partial(gather_kernel, order, rest), in_specs=[V...]
    unnamed x120 -> x114, local copies, waits for them, and re-layouts: 21.2 us -> 31 us
    all_to_all x4, waiting for transfers between devices: 14.7 us -> 5.97 us  [cube_exchange(): lax.all_to_all(blocks, ('bias', 'low', 'rest'), split_axis=0, concat_axis...]
    all_to_all x11 -> x12, starting transfers between devices: 55.6 us -> 60.6 us  [plane_exchange(): lax.all_to_all(blocks, ('bias', 'rest'), split_axis=0, concat_axis=0, til...]
    all_to_all x11 -> x12, waiting for transfers between devices: 43.5 us -> 41.3 us  [plane_exchange(): lax.all_to_all(blocks, ('bias', 'rest'), split_axis=0, concat_axis=0, til...]
  transfers between devices with their start and end apart: 43 -> 44, of which waited for: 20 -> 21; matrix products, arithmetic and copies ran while one was open for 8% -> 10% of each run, Pallas kernels for 11% -> 14%
where the time goes in v3:
time: 624 us; the launch traced here: 619 us
  waiting for transfers between devices  303 us (49%)
  Pallas kernels  124 us (20%)
  starting transfers between devices  119 us (19%)
  local copies, waits for them, and re-layouts  59.9 us (10%)
  other arithmetic  12.7 us (2%)
    ppermute x28, waiting for transfers between devices, turn(): lax.ppermute(blocks, ('half', 'low'), [(i, i ^ step) for i in range(4)])  256 us
    all_to_all x12, starting transfers between devices, plane_exchange(): lax.all_to_all(blocks, ('bias', 'rest'), split_axis=0, concat_axis=0, til...  60.6 us
    all_to_all x12, waiting for transfers between devices, plane_exchange(): lax.all_to_all(blocks, ('bias', 'rest'), split_axis=0, concat_axis=0, til...  41.3 us
    ppermute x28, starting transfers between devices, turn(): lax.ppermute(blocks, ('half', 'low'), [(i, i ^ step) for i in range(4)])  38.5 us
    unnamed x114, local copies, waits for them, and re-layouts  31 us
    pallas_call x4, Pallas kernels, polarization(): pl.pallas_call(polar_kernel, in_specs=[VMEM] * 7, out_specs=[VMEM] * 2, o...  29.2 us
    pallas_call x4, Pallas kernels, self_energy(): pl.pallas_call(fold_kernel, in_specs=[SMEM] + [VMEM] * 4, out_specs=[VMEM...  27.3 us
    pallas_call x1, Pallas kernels, screened(): pl.pallas_call(screen_kernel, in_specs=[SMEM] + [VMEM] * (2 + CHUNKS), ou...  20.3 us
  transfers between devices with their start and end apart: 44, of which 21 were waited for; matrix products, arithmetic and copies ran while one was open for 10% of the time, Pallas kernels for 14%

profile of v3, /device:TPU:1, one launch (start us, length us, event | category | flops | bytes accessed | tf_op | source)
XLA Modules:
  0.0 619.0 jit_solution(6255386380803331182)
XLA Ops:
  5.8 5.4 all-to-all-start.6
  50.3 15.7 %all-to-all-done.2 = bf16[8,2,2,2,4,16,256]{6,5,4,3,2,1,0:T(8,128)(2,1)} async-done(((bf16[8,2,2,2,4,16,256]{6,5,4,3,2,1,0:T(8,128)(2,1)}), bf16[8,2,2,2,4,16,256]{6,5,4,3,2,1,0:T(8,128)(2,1)}, u32[]{:S(2)}, u32[]{:S(2)}) %all-to-all-start.2) | async-done | bytes 2097184 | tf_op jit(solution)/shard_map/all_to_all | solution.py:557
  80.1 15.9 %all-to-all-done.4 = bf16[8,2,2,2,4,16,256]{6,5,4,3,2,1,0:T(8,128)(2,1)} async-done(((bf16[8,2,2,2,4,16,256]{6,5,4,3,2,1,0:T(8,128)(2,1)}), bf16[8,2,2,2,4,16,256]{6,5,4,3,2,1,0:T(8,128)(2,1)}, u32[]{:S(2)}, u32[]{:S(2)}) %all-to-all-start.4) | async-done | bytes 2097184 | tf_op jit(solution)/shard_map/all_to_all | solution.py:557
  123.3 32.7 %collective-permute-done.4.refs_2_ = bf16[4,2,2,4,16,256]{5,4,3,2,1,0:T(8,128)(2,1)} collective-permute-done((bf16[4,2,2,4,16,256]{5,4,3,2,1,0:T(8,128)(2,1)}, bf16[4,2,2,4,16,256]{5,4,3,2,1,0:T(8,128)(2,1)}, u32[]{:S(2)}, u32[]{:S(2)}) %collective-permute-start.4) | collective-permute-done | bytes 524320 | tf_op jit(solution)/shard_map/ppermute | solution.py:561
  156.0 7.3 %polarization.5 = (bf16[16,2,4,16,256]{4,3,2,1,0:T(8,128)(2,1)}, bf16[2,1024,512]{2,1,0:T(8,128)(2,1)}) custom-call(bf16[1024,512]{1,0:T(8,128)(2,1)} %copy.11.minus_ref, bf16[1024,512]{1,0:T(8,128)(2,1)} %copy.12.plus_ref, bf16[512,1024]{1,0:T(8,128)(2,1)} %fusion.back_ref, bf16[4,2,2,4,16,256]{5,4,3,2,1,0:T(8,128)(2,1)} %get-tuple-element.102.refs_0_, ...), custom_call_target="tpu_custom_call" | custom-call | flops 3221225472 | bytes 5242880 | tf_op jit(solution)/shard_map/polarization/pallas_call | solution.py:192
  174.2 20.7 %collective-permute-done.8.refs_3_ = bf16[4,2,2,4,16,256]{5,4,3,2,1,0:T(8,128)(2,1)S(1)} collective-permute-done((bf16[4,2,2,4,16,256]{5,4,3,2,1,0:T(8,128)(2,1)S(1)}, bf16[4,2,2,4,16,256]{5,4,3,2,1,0:T(8,128)(2,1)S(1)}, u32[]{:S(2)}, u32[]{:S(2)}) %collective-permute-start.8) | collective-permute-done | bytes 524320 | tf_op jit(solution)/shard_map/ppermute | solution.py:561
  194.9 23.6 %collective-permute-done.7.refs_2_ = bf16[4,2,2,4,16,256]{5,4,3,2,1,0:T(8,128)(2,1)S(1)} collective-permute-done((bf16[4,2,2,4,16,256]{5,4,3,2,1,0:T(8,128)(2,1)S(1)}, bf16[4,2,2,4,16,256]{5,4,3,2,1,0:T(8,128)(2,1)S(1)}, u32[]{:S(2)}, u32[]{:S(2)}) %collective-permute-start.7) | collective-permute-done | bytes 524320 | tf_op jit(solution)/shard_map/ppermute | solution.py:561
  220.1 7.3 %polarization.6 = (bf16[16,2,4,16,256]{4,3,2,1,0:T(8,128)(2,1)}, bf16[2,1024,512]{2,1,0:T(8,128)(2,1)}) custom-call(bf16[1024,512]{1,0:T(8,128)(2,1)} %copy.11.minus_ref, bf16[1024,512]{1,0:T(8,128)(2,1)} %copy.12.plus_ref, bf16[512,1024]{1,0:T(8,128)(2,1)} %fusion.back_ref, bf16[4,2,2,4,16,256]{5,4,3,2,1,0:T(8,128)(2,1)} %get-tuple-element.98.refs_0_, ...), custom_call_target="tpu_custom_call" | custom-call | flops 3221225472 | bytes 5242880 | tf_op jit(solution)/shard_map/polarization/pallas_call | solution.py:192
  227.4 5.3 all-to-all-start.5
  238.8 20.3 %collective-permute-done.2.refs_3_ = bf16[4,2,2,4,16,256]{5,4,3,2,1,0:T(8,128)(2,1)S(1)} collective-permute-done((bf16[4,2,2,4,16,256]{5,4,3,2,1,0:T(8,128)(2,1)S(1)}, bf16[4,2,2,4,16,256]{5,4,3,2,1,0:T(8,128)(2,1)S(1)}, u32[]{:S(2)}, u32[]{:S(2)}) %collective-permute-start.2) | collective-permute-done | bytes 524320 | tf_op jit(solution)/shard_map/ppermute | solution.py:561
  259.1 24.0 %collective-permute-done.1.refs_2_ = bf16[4,2,2,4,16,256]{5,4,3,2,1,0:T(8,128)(2,1)S(1)} collective-permute-done((bf16[4,2,2,4,16,256]{5,4,3,2,1,0:T(8,128)(2,1)S(1)}, bf16[4,2,2,4,16,256]{5,4,3,2,1,0:T(8,128)(2,1)S(1)}, u32[]{:S(2)}, u32[]{:S(2)}) %collective-permute-start.1) | collective-permute-done | bytes 524320 | tf_op jit(solution)/shard_map/ppermute | solution.py:561
  284.1 7.3 %polarization.4 = (bf16[16,2,4,16,256]{4,3,2,1,0:T(8,128)(2,1)}, bf16[2,1024,512]{2,1,0:T(8,128)(2,1)}) custom-call(bf16[1024,512]{1,0:T(8,128)(2,1)} %copy.11.minus_ref, bf16[1024,512]{1,0:T(8,128)(2,1)} %copy.12.plus_ref, bf16[512,1024]{1,0:T(8,128)(2,1)} %fusion.back_ref, bf16[4,2,2,4,16,256]{5,4,3,2,1,0:T(8,128)(2,1)} %get-tuple-element.106.refs_0_, ...), custom_call_target="tpu_custom_call" | custom-call | flops 3221225472 | bytes 5242880 | tf_op jit(solution)/shard_map/polarization/pallas_call | solution.py:192
  300.9 21.7 %collective-permute-done.11.refs_3_ = bf16[4,2,2,4,16,256]{5,4,3,2,1,0:T(8,128)(2,1)S(1)} collective-permute-done((bf16[4,2,2,4,16,256]{5,4,3,2,1,0:T(8,128)(2,1)S(1)}, bf16[4,2,2,4,16,256]{5,4,3,2,1,0:T(8,128)(2,1)S(1)}, u32[]{:S(2)}, u32[]{:S(2)}) %collective-permute-start.11) | collective-permute-done | bytes 524320 | tf_op jit(solution)/shard_map/ppermute | solution.py:561
  322.6 22.6 %collective-permute-done.10.refs_2_ = bf16[4,2,2,4,16,256]{5,4,3,2,1,0:T(8,128)(2,1)S(1)} collective-permute-done((bf16[4,2,2,4,16,256]{5,4,3,2,1,0:T(8,128)(2,1)S(1)}, bf16[4,2,2,4,16,256]{5,4,3,2,1,0:T(8,128)(2,1)S(1)}, u32[]{:S(2)}, u32[]{:S(2)}) %collective-permute-start.10) | collective-permute-done | bytes 524320 | tf_op jit(solution)/shard_map/ppermute | solution.py:561
  346.2 7.3 %polarization.7 = (bf16[16,2,4,16,256]{4,3,2,1,0:T(8,128)(2,1)}, bf16[2,1024,512]{2,1,0:T(8,128)(2,1)}) custom-call(bf16[1024,512]{1,0:T(8,128)(2,1)} %copy.11.minus_ref, bf16[1024,512]{1,0:T(8,128)(2,1)} %copy.12.plus_ref, bf16[512,1024]{1,0:T(8,128)(2,1)} %fusion.back_ref, bf16[4,2,2,4,16,256]{5,4,3,2,1,0:T(8,128)(2,1)} %get-tuple-element.94.refs_0_, ...), custom_call_target="tpu_custom_call" | custom-call | flops 3221225472 | bytes 5242880 | tf_op jit(solution)/shard_map/polarization/pallas_call | solution.py:192
  367.7 6.0 all-to-all-done.7.refs_3_
  374.7 20.3 %screened.1 = (bf16[8,2,2,4,16,256]{5,4,3,2,1,0:T(8,128)(2,1)}, bf16[8,2,2,4,16,256]{5,4,3,2,1,0:T(8,128)(2,1)}, bf16[8,2,2,4,16,256]{5,4,3,2,1,0:T(8,128)(2,1)}...) custom-call(s32[2]{0:T(128)} %pad_add_fusion.place_ref, ...), custom_call_target="tpu_custom_call" | custom-call | flops 5368709120 | bytes 8388608 | tf_op jit(solution)/shard_map/screened/pallas_call | solution.py:374
  395.0 12.7 %collective-permute-done.12 = bf16[8,2,4,16,256]{4,3,2,1,0:T(8,128)(2,1)S(1)} collective-permute-done((bf16[8,2,4,16,256]{4,3,2,1,0:T(8,128)(2,1)}, bf16[8,2,4,16,256]{4,3,2,1,0:T(8,128)(2,1)S(1)}, u32[]{:S(2)}, u32[]{:S(2)}) %collective-permute-start.12) | collective-permute-done | bytes 524320 | tf_op jit(solution)/shard_map/ppermute | solution.py:561
  408.6 5.3 all-to-all-start.8
  413.9 13.3 %collective-permute-done.16 = bf16[8,2,4,16,256]{4,3,2,1,0:T(8,128)(2,1)S(1)} collective-permute-done((bf16[8,2,4,16,256]{4,3,2,1,0:T(8,128)(2,1)S(1)}, bf16[8,2,4,16,256]{4,3,2,1,0:T(8,128)(2,1)S(1)}, u32[]{:S(2)}, u32[]{:S(2)}) %collective-permute-start.16) | collective-permute-done | bytes 524320 | tf_op jit(solution)/shard_map/ppermute | solution.py:561
  432.9 13.6 %collective-permute-done.20 = bf16[8,2,4,16,256]{4,3,2,1,0:T(8,128)(2,1)S(1)} collective-permute-done((bf16[8,2,4,16,256]{4,3,2,1,0:T(8,128)(2,1)}, bf16[8,2,4,16,256]{4,3,2,1,0:T(8,128)(2,1)S(1)}, u32[]{:S(2)}, u32[]{:S(2)}) %collective-permute-start.20) | collective-permute-done | bytes 524320 | tf_op jit(solution)/shard_map/ppermute | solution.py:561
  454.4 6.8 %self_energy.4 = (bf16[2,4,2,2,4,16,256]{6,5,4,3,2,1,0:T(8,128)(2,1)}, bf16[4,2,4,16,256]{4,3,2,1,0:T(8,128)(2,1)}, bf16[4,2,4,16,256]{4,3,2,1,0:T(8,128)(2,1)}, bf16[4,2,4,16,256]{4,3,2,1,0:T(8,128)(2,1)}) custom-call(s32[2]{0:T(128)} %pad_add_fusion.place_ref, bf16[1024,512]{1,0:T(8,128)(2,1)} %copy.31.minus_ref, ...), custom_call_target="tpu_custom_call" | custom-call | flops 2147483648 | bytes 4194304 | tf_op jit(solution)/shard_map/self_energy/pallas_call | solution.py:241
  467.6 5.5 all-to-all-start.14
  475.2 6.8 %self_energy.5 = (bf16[2,4,2,2,4,16,256]{6,5,4,3,2,1,0:T(8,128)(2,1)}, bf16[4,2,4,16,256]{4,3,2,1,0:T(8,128)(2,1)}, bf16[4,2,4,16,256]{4,3,2,1,0:T(8,128)(2,1)}, bf16[4,2,4,16,256]{4,3,2,1,0:T(8,128)(2,1)}) custom-call(s32[2]{0:T(128)} %pad_add_fusion.place_ref, bf16[1024,512]{1,0:T(8,128)(2,1)} %copy.31.minus_ref, ...), custom_call_target="tpu_custom_call" | custom-call | flops 2147483648 | bytes 4194304 | tf_op jit(solution)/shard_map/self_energy/pallas_call | solution.py:241
  483.6 10.0 %collective-permute-done.14 = bf16[4,2,4,16,256]{4,3,2,1,0:T(8,128)(2,1)} collective-permute-done((bf16[4,2,4,16,256]{4,3,2,1,0:T(8,128)(2,1)}, bf16[4,2,4,16,256]{4,3,2,1,0:T(8,128)(2,1)}, u32[]{:S(2)}, u32[]{:S(2)}) %collective-permute-start.14) | collective-permute-done | bytes 262176 | tf_op jit(solution)/shard_map/ppermute | solution.py:561
  500.9 5.3 collective-permute-start.18
  507.8 6.9 %self_energy.6 = (bf16[2,4,2,2,4,16,256]{6,5,4,3,2,1,0:T(8,128)(2,1)}, bf16[4,2,4,16,256]{4,3,2,1,0:T(8,128)(2,1)}, bf16[4,2,4,16,256]{4,3,2,1,0:T(8,128)(2,1)}, bf16[4,2,4,16,256]{4,3,2,1,0:T(8,128)(2,1)}) custom-call(s32[2]{0:T(128)} %pad_add_fusion.place_ref, bf16[1024,512]{1,0:T(8,128)(2,1)} %copy.31.minus_ref, ...), custom_call_target="tpu_custom_call" | custom-call | flops 2147483648 | bytes 4194304 | tf_op jit(solution)/shard_map/self_energy/pallas_call | solution.py:241
  514.7 9.8 %collective-permute-done.18 = bf16[4,2,4,16,256]{4,3,2,1,0:T(8,128)(2,1)} collective-permute-done((bf16[4,2,4,16,256]{4,3,2,1,0:T(8,128)(2,1)}, bf16[4,2,4,16,256]{4,3,2,1,0:T(8,128)(2,1)}, u32[]{:S(2)}, u32[]{:S(2)}) %collective-permute-start.18) | collective-permute-done | bytes 262176 | tf_op jit(solution)/shard_map/ppermute | solution.py:561
  538.8 6.8 %self_energy.7 = (bf16[2,4,2,2,4,16,256]{6,5,4,3,2,1,0:T(8,128)(2,1)}, bf16[4,2,4,16,256]{4,3,2,1,0:T(8,128)(2,1)}, bf16[4,2,4,16,256]{4,3,2,1,0:T(8,128)(2,1)}, bf16[4,2,4,16,256]{4,3,2,1,0:T(8,128)(2,1)}) custom-call(s32[2]{0:T(128)} %pad_add_fusion.place_ref, bf16[1024,512]{1,0:T(8,128)(2,1)} %copy.31.minus_ref, ...), custom_call_target="tpu_custom_call" | custom-call | flops 2147483648 | bytes 4194304 | tf_op jit(solution)/shard_map/self_energy/pallas_call | solution.py:241
  546.5 8.8 %collective-permute-done.22 = bf16[4,2,4,16,256]{4,3,2,1,0:T(8,128)(2,1)S(1)} collective-permute-done((bf16[4,2,4,16,256]{4,3,2,1,0:T(8,128)(2,1)}, bf16[4,2,4,16,256]{4,3,2,1,0:T(8,128)(2,1)S(1)}, u32[]{:S(2)}, u32[]{:S(2)}) %collective-permute-start.22) | collective-permute-done | bytes 262176 | tf_op jit(solution)/shard_map/ppermute | solution.py:561
  569.1 15.8 %collective-permute-done.26 = bf16[4,2,4,16,256]{4,3,2,1,0:T(8,128)(2,1)S(1)} collective-permute-done((bf16[4,2,4,16,256]{4,3,2,1,0:T(8,128)(2,1)}, bf16[4,2,4,16,256]{4,3,2,1,0:T(8,128)(2,1)S(1)}, u32[]{:S(2)}, u32[]{:S(2)}) %collective-permute-start.26) | collective-permute-done | bytes 262176 | tf_op jit(solution)/shard_map/ppermute | solution.py:561
  605.9 13.1 %dyson.1 = bf16[16,2,256,256]{3,2,1,0:T(8,128)(2,1)} custom-call(bf16[256,256]{1,0:T(8,128)(2,1)} %fusion.1.swap_ref, bf16[16,2,4,16,256]{4,3,2,1,0:T(8,128)(2,1)} %gathered.9.refs_0_, bf16[16,2,4,16,256]{4,3,2,1,0:T(8,128)(2,1)} %gathered.10.refs_1_, bf16[16,2,4,16,256]{4,3,2,1,0:T(8,128)(2,1)} %gathered.11.refs_2_, ...), custom_call_target="tpu_custom_call" | custom-call | flops 4831838208 | bytes 12582912 | tf_op jit(solution)/shard_map/dyson/pallas_call | solution.py:420
  (233 shorter events, 214.7 us)
Async XLA Ops:
  5.8 30.1 %all-to-all-start.6 = ((bf16[8,2,2,2,4,16,256]{6,5,4,3,2,1,0:T(8,128)(2,1)}), bf16[8,2,2,2,4,16,256]{6,5,4,3,2,1,0:T(8,128)(2,1)S(1)}, u32[]{:S(2)}, u32[]{:S(2)}) async-start(bf16[8,2,2,2,4,16,256]{6,5,4,3,2,1,0:T(8,128)(2,1)} %pack.7), calls=%async_computation.6 | async-start | bytes 4194304 | tf_op jit(solution)/shard_map/all_to_all | solution.py:557
  35.9 30.1 %all-to-all-start.2 = ((bf16[8,2,2,2,4,16,256]{6,5,4,3,2,1,0:T(8,128)(2,1)}), bf16[8,2,2,2,4,16,256]{6,5,4,3,2,1,0:T(8,128)(2,1)}, u32[]{:S(2)}, u32[]{:S(2)}) async-start(bf16[8,2,2,2,4,16,256]{6,5,4,3,2,1,0:T(8,128)(2,1)} %pack.5), calls=%async_computation.2 | async-start | bytes 4194304 | tf_op jit(solution)/shard_map/all_to_all | solution.py:557
  66.0 30.1 %all-to-all-start.4 = ((bf16[8,2,2,2,4,16,256]{6,5,4,3,2,1,0:T(8,128)(2,1)}), bf16[8,2,2,2,4,16,256]{6,5,4,3,2,1,0:T(8,128)(2,1)}, u32[]{:S(2)}, u32[]{:S(2)}) async-start(bf16[8,2,2,2,4,16,256]{6,5,4,3,2,1,0:T(8,128)(2,1)} %pack.6), calls=%async_computation.4 | async-start | bytes 4194304 | tf_op jit(solution)/shard_map/all_to_all | solution.py:557
  96.0 67.3 %all-to-all-start = ((bf16[8,2,2,2,4,16,256]{6,5,4,3,2,1,0:T(8,128)(2,1)}), bf16[8,2,2,2,4,16,256]{6,5,4,3,2,1,0:T(8,128)(2,1)}, u32[]{:S(2)}, u32[]{:S(2)}) async-start(bf16[8,2,2,2,4,16,256]{6,5,4,3,2,1,0:T(8,128)(2,1)} %pack.4), calls=%async_computation | async-start | bytes 4194304 | tf_op jit(solution)/shard_map/all_to_all | solution.py:557
  111.0 45.1 %collective-permute-start.4 = (bf16[4,2,2,4,16,256]{5,4,3,2,1,0:T(8,128)(2,1)}, bf16[4,2,2,4,16,256]{5,4,3,2,1,0:T(8,128)(2,1)}, u32[]{:S(2)}, u32[]{:S(2)}) collective-permute-start(bf16[4,2,2,4,16,256]{5,4,3,2,1,0:T(8,128)(2,1)} %get-tuple-element.100), channel_id=1, source_target_pairs={{0,8},{4,12},{8,0},{12,4},{1,9},{5,13},{9,1},{13,5},{2,10},{6,14},... | collective-permute-start | bytes 1572872 | tf_op jit(solution)/shard_map/ppermute | solution.py:561
  111.0 45.1 %collective-permute-start.3 = (bf16[4,2,2,4,16,256]{5,4,3,2,1,0:T(8,128)(2,1)}, bf16[4,2,2,4,16,256]{5,4,3,2,1,0:T(8,128)(2,1)}, u32[]{:S(2)}, u32[]{:S(2)}) collective-permute-start(bf16[4,2,2,4,16,256]{5,4,3,2,1,0:T(8,128)(2,1)} %get-tuple-element.101), channel_id=1, source_target_pairs={{0,4},{4,0},{8,12},{12,8},{1,5},{5,1},{9,13},{13,9},{2,6},{6,2},{1... | collective-permute-start | bytes 1572872 | tf_op jit(solution)/shard_map/ppermute | solution.py:561
  163.3 64.1 %all-to-all-start.3 = ((bf16[16,2,4,16,256]{4,3,2,1,0:T(8,128)(2,1)}), bf16[16,2,4,16,256]{4,3,2,1,0:T(8,128)(2,1)S(1)}, u32[]{:S(2)}, u32[]{:S(2)}) async-start(bf16[16,2,4,16,256]{4,3,2,1,0:T(8,128)(2,1)} %get-tuple-element.53), calls=%async_computation.3 | async-start | bytes 2097152 | tf_op jit(solution)/shard_map/all_to_all | solution.py:553
  170.7 24.3 %collective-permute-start.8 = (bf16[4,2,2,4,16,256]{5,4,3,2,1,0:T(8,128)(2,1)S(1)}, bf16[4,2,2,4,16,256]{5,4,3,2,1,0:T(8,128)(2,1)S(1)}, u32[]{:S(2)}, u32[]{:S(2)}) collective-permute-start(bf16[4,2,2,4,16,256]{5,4,3,2,1,0:T(8,128)(2,1)S(1)} %get-tuple-element.95), channel_id=1, source_target_pairs={{0,12},{4,8},{8,4},{12,0},{1,13},{5,9},{9,5},{13,1},{2,14},{6,10},... | collective-permute-start | bytes 1572872 | tf_op jit(solution)/shard_map/ppermute | solution.py:561
  173.9 44.6 %collective-permute-start.7 = (bf16[4,2,2,4,16,256]{5,4,3,2,1,0:T(8,128)(2,1)S(1)}, bf16[4,2,2,4,16,256]{5,4,3,2,1,0:T(8,128)(2,1)S(1)}, u32[]{:S(2)}, u32[]{:S(2)}) collective-permute-start(bf16[4,2,2,4,16,256]{5,4,3,2,1,0:T(8,128)(2,1)S(1)} %get-tuple-element.96), channel_id=1, source_target_pairs={{0,8},{4,12},{8,0},{12,4},{1,9},{5,13},{9,1},{13,5},{2,10},{6,14},... | collective-permute-start | bytes 1572872 | tf_op jit(solution)/shard_map/ppermute | solution.py:561
  173.9 44.6 %collective-permute-start.6 = (bf16[4,2,2,4,16,256]{5,4,3,2,1,0:T(8,128)(2,1)S(1)}, bf16[4,2,2,4,16,256]{5,4,3,2,1,0:T(8,128)(2,1)S(1)}, u32[]{:S(2)}, u32[]{:S(2)}) collective-permute-start(bf16[4,2,2,4,16,256]{5,4,3,2,1,0:T(8,128)(2,1)S(1)} %get-tuple-element.97), channel_id=1, source_target_pairs={{0,4},{4,0},{8,12},{12,8},{1,5},{5,1},{9,13},{13,9},{2,6},{6,2},{1... | collective-permute-start | bytes 1572872 | tf_op jit(solution)/shard_map/ppermute | solution.py:561
  227.4 64.0 %all-to-all-start.5 = ((bf16[16,2,4,16,256]{4,3,2,1,0:T(8,128)(2,1)}), bf16[16,2,4,16,256]{4,3,2,1,0:T(8,128)(2,1)}, u32[]{:S(2)}, u32[]{:S(2)}) async-start(bf16[16,2,4,16,256]{4,3,2,1,0:T(8,128)(2,1)} %get-tuple-element.54), calls=%async_computation.5 | async-start | bytes 2097152 | tf_op jit(solution)/shard_map/all_to_all | solution.py:553
  235.2 23.9 %collective-permute-start.2 = (bf16[4,2,2,4,16,256]{5,4,3,2,1,0:T(8,128)(2,1)S(1)}, bf16[4,2,2,4,16,256]{5,4,3,2,1,0:T(8,128)(2,1)S(1)}, u32[]{:S(2)}, u32[]{:S(2)}) collective-permute-start(bf16[4,2,2,4,16,256]{5,4,3,2,1,0:T(8,128)(2,1)S(1)} %get-tuple-element.103), channel_id=1, source_target_pairs={{0,12},{4,8},{8,4},{12,0},{1,13},{5,9},{9,5},{13,1},{2,14},{6,10},... | collective-permute-start | bytes 1572872 | tf_op jit(solution)/shard_map/ppermute | solution.py:561
  238.1 45.0 %collective-permute-start.1 = (bf16[4,2,2,4,16,256]{5,4,3,2,1,0:T(8,128)(2,1)S(1)}, bf16[4,2,2,4,16,256]{5,4,3,2,1,0:T(8,128)(2,1)S(1)}, u32[]{:S(2)}, u32[]{:S(2)}) collective-permute-start(bf16[4,2,2,4,16,256]{5,4,3,2,1,0:T(8,128)(2,1)S(1)} %get-tuple-element.104), channel_id=1, source_target_pairs={{0,8},{4,12},{8,0},{12,4},{1,9},{5,13},{9,1},{13,5},{2,10},{6,14},... | collective-permute-start | bytes 1572872 | tf_op jit(solution)/shard_map/ppermute | solution.py:561
  238.1 45.0 %collective-permute-start = (bf16[4,2,2,4,16,256]{5,4,3,2,1,0:T(8,128)(2,1)S(1)}, bf16[4,2,2,4,16,256]{5,4,3,2,1,0:T(8,128)(2,1)S(1)}, u32[]{:S(2)}, u32[]{:S(2)}) collective-permute-start(bf16[4,2,2,4,16,256]{5,4,3,2,1,0:T(8,128)(2,1)S(1)} %get-tuple-element.105), channel_id=1, source_target_pairs={{0,4},{4,0},{8,12},{12,8},{1,5},{5,1},{9,13},{13,9},{2,6},{6,2},{1... | collective-permute-start | bytes 1572872 | tf_op jit(solution)/shard_map/ppermute | solution.py:561
  291.4 62.1 %all-to-all-start.1 = ((bf16[16,2,4,16,256]{4,3,2,1,0:T(8,128)(2,1)}), bf16[16,2,4,16,256]{4,3,2,1,0:T(8,128)(2,1)S(1)}, u32[]{:S(2)}, u32[]{:S(2)}) async-start(bf16[16,2,4,16,256]{4,3,2,1,0:T(8,128)(2,1)} %get-tuple-element.52), calls=%async_computation.1 | async-start | bytes 2097152 | tf_op jit(solution)/shard_map/all_to_all | solution.py:553
  297.3 25.3 %collective-permute-start.11 = (bf16[4,2,2,4,16,256]{5,4,3,2,1,0:T(8,128)(2,1)S(1)}, bf16[4,2,2,4,16,256]{5,4,3,2,1,0:T(8,128)(2,1)S(1)}, u32[]{:S(2)}, u32[]{:S(2)}) collective-permute-start(bf16[4,2,2,4,16,256]{5,4,3,2,1,0:T(8,128)(2,1)S(1)} %get-tuple-element.91), channel_id=1, source_target_pairs={{0,12},{4,8},{8,4},{12,0},{1,13},{5,9},{9,5},{13,1},{2,14},{6,10},... | collective-permute-start | bytes 1572872 | tf_op jit(solution)/shard_map/ppermute | solution.py:561
  300.1 45.1 %collective-permute-start.10 = (bf16[4,2,2,4,16,256]{5,4,3,2,1,0:T(8,128)(2,1)S(1)}, bf16[4,2,2,4,16,256]{5,4,3,2,1,0:T(8,128)(2,1)S(1)}, u32[]{:S(2)}, u32[]{:S(2)}) collective-permute-start(bf16[4,2,2,4,16,256]{5,4,3,2,1,0:T(8,128)(2,1)S(1)} %get-tuple-element.92), channel_id=1, source_target_pairs={{0,8},{4,12},{8,0},{12,4},{1,9},{5,13},{9,1},{13,5},{2,10},{6,14},... | collective-permute-start | bytes 1572872 | tf_op jit(solution)/shard_map/ppermute | solution.py:561
  300.1 45.1 %collective-permute-start.9 = (bf16[4,2,2,4,16,256]{5,4,3,2,1,0:T(8,128)(2,1)S(1)}, bf16[4,2,2,4,16,256]{5,4,3,2,1,0:T(8,128)(2,1)S(1)}, u32[]{:S(2)}, u32[]{:S(2)}) collective-permute-start(bf16[4,2,2,4,16,256]{5,4,3,2,1,0:T(8,128)(2,1)S(1)} %get-tuple-element.93), channel_id=1, source_target_pairs={{0,4},{4,0},{8,12},{12,8},{1,5},{5,1},{9,13},{13,9},{2,6},{6,2},{1... | collective-permute-start | bytes 1572872 | tf_op jit(solution)/shard_map/ppermute | solution.py:561
  353.5 20.2 %all-to-all-start.7 = ((bf16[16,2,4,16,256]{4,3,2,1,0:T(8,128)(2,1)}), bf16[16,2,4,16,256]{4,3,2,1,0:T(8,128)(2,1)S(1)}, u32[]{:S(2)}, u32[]{:S(2)}) async-start(bf16[16,2,4,16,256]{4,3,2,1,0:T(8,128)(2,1)} %get-tuple-element.55), calls=%async_computation.7 | async-start | bytes 2097152 | tf_op jit(solution)/shard_map/all_to_all | solution.py:553
  461.2 21.5 %collective-permute-start.13 = (bf16[4,2,4,16,256]{4,3,2,1,0:T(8,128)(2,1)}, bf16[4,2,4,16,256]{4,3,2,1,0:T(8,128)(2,1)}, u32[]{:S(2)}, u32[]{:S(2)}) collective-permute-start(bf16[4,2,4,16,256]{4,3,2,1,0:T(8,128)(2,1)} %get-tuple-element.59), channel_id=1, source_target_pairs={{0,4},{4,0},{8,12},{12,8},{1,5},{5,1},{9,13},{13,9},{2,6},{6,2},{1... | collective-permute-start | bytes 786440 | tf_op jit(solution)/shard_map/ppermute | solution.py:561
  467.6 28.0 %all-to-all-start.14 = ((bf16[8,2,2,4,16,256]{5,4,3,2,1,0:T(8,128)(2,1)}), bf16[8,2,2,4,16,256]{5,4,3,2,1,0:T(8,128)(2,1)S(1)}, u32[]{:S(2)}, u32[]{:S(2)}) async-start(bf16[8,2,2,4,16,256]{5,4,3,2,1,0:T(8,128)(2,1)} %bitcast_dynamic-update-slice_fusion), calls=%async_computation.14 | async-start | bytes 2097152 | tf_op jit(solution)/shard_map/all_to_all | solution.py:557
  473.1 20.5 %collective-permute-start.14 = (bf16[4,2,4,16,256]{4,3,2,1,0:T(8,128)(2,1)}, bf16[4,2,4,16,256]{4,3,2,1,0:T(8,128)(2,1)}, u32[]{:S(2)}, u32[]{:S(2)}) collective-permute-start(bf16[4,2,4,16,256]{4,3,2,1,0:T(8,128)(2,1)} %get-tuple-element.60), channel_id=1, source_target_pairs={{0,8},{4,12},{8,0},{12,4},{1,9},{5,13},{9,1},{13,5},{2,10},{6,14},... | collective-permute-start | bytes 786440 | tf_op jit(solution)/shard_map/ppermute | solution.py:561
  474.8 19.8 %collective-permute-start.15 = (bf16[4,2,4,16,256]{4,3,2,1,0:T(8,128)(2,1)}, bf16[4,2,4,16,256]{4,3,2,1,0:T(8,128)(2,1)}, u32[]{:S(2)}, u32[]{:S(2)}) collective-permute-start(bf16[4,2,4,16,256]{4,3,2,1,0:T(8,128)(2,1)} %get-tuple-element.61), channel_id=1, source_target_pairs={{0,12},{4,8},{8,4},{12,0},{1,13},{5,9},{9,5},{13,1},{2,14},{6,10},... | collective-permute-start | bytes 786440 | tf_op jit(solution)/shard_map/ppermute | solution.py:561
  482.0 32.6 %collective-permute-start.17 = (bf16[4,2,4,16,256]{4,3,2,1,0:T(8,128)(2,1)}, bf16[4,2,4,16,256]{4,3,2,1,0:T(8,128)(2,1)S(1)}, u32[]{:S(2)}, u32[]{:S(2)}) collective-permute-start(bf16[4,2,4,16,256]{4,3,2,1,0:T(8,128)(2,1)} %get-tuple-element.66), channel_id=1, source_target_pairs={{0,4},{4,0},{8,12},{12,8},{1,5},{5,1},{9,13},{13,9},{2,6},{6,2},{1... | collective-permute-start | bytes 786440 | tf_op jit(solution)/shard_map/ppermute | solution.py:561
  496.6 29.9 %all-to-all-start.9 = ((bf16[8,2,2,4,16,256]{5,4,3,2,1,0:T(8,128)(2,1)}), bf16[8,2,2,4,16,256]{5,4,3,2,1,0:T(8,128)(2,1)S(1)}, u32[]{:S(2)}, u32[]{:S(2)}) async-start(bf16[8,2,2,4,16,256]{5,4,3,2,1,0:T(8,128)(2,1)} %bitcast.136), calls=%async_computation.9 | async-start | bytes 2097152 | tf_op jit(solution)/shard_map/all_to_all | solution.py:557
  500.9 23.6 %collective-permute-start.18 = (bf16[4,2,4,16,256]{4,3,2,1,0:T(8,128)(2,1)}, bf16[4,2,4,16,256]{4,3,2,1,0:T(8,128)(2,1)}, u32[]{:S(2)}, u32[]{:S(2)}) collective-permute-start(bf16[4,2,4,16,256]{4,3,2,1,0:T(8,128)(2,1)} %get-tuple-element.67), channel_id=1, source_target_pairs={{0,8},{4,12},{8,0},{12,4},{1,9},{5,13},{9,1},{13,5},{2,10},{6,14},... | collective-permute-start | bytes 786440 | tf_op jit(solution)/shard_map/ppermute | solution.py:561
  514.7 31.0 %collective-permute-start.21 = (bf16[4,2,4,16,256]{4,3,2,1,0:T(8,128)(2,1)}, bf16[4,2,4,16,256]{4,3,2,1,0:T(8,128)(2,1)S(1)}, u32[]{:S(2)}, u32[]{:S(2)}) collective-permute-start(bf16[4,2,4,16,256]{4,3,2,1,0:T(8,128)(2,1)} %get-tuple-element.73), channel_id=1, source_target_pairs={{0,4},{4,0},{8,12},{12,8},{1,5},{5,1},{9,13},{13,9},{2,6},{6,2},{1... | collective-permute-start | bytes 786440 | tf_op jit(solution)/shard_map/ppermute | solution.py:561
  527.4 29.3 %all-to-all-start.11 = ((bf16[8,2,2,4,16,256]{5,4,3,2,1,0:T(8,128)(2,1)}), bf16[8,2,2,4,16,256]{5,4,3,2,1,0:T(8,128)(2,1)S(1)}, u32[]{:S(2)}, u32[]{:S(2)}) async-start(bf16[8,2,2,4,16,256]{5,4,3,2,1,0:T(8,128)(2,1)} %bitcast.135), calls=%async_computation.11 | async-start | bytes 2097152 | tf_op jit(solution)/shard_map/all_to_all | solution.py:557
  532.4 22.8 %collective-permute-start.22 = (bf16[4,2,4,16,256]{4,3,2,1,0:T(8,128)(2,1)}, bf16[4,2,4,16,256]{4,3,2,1,0:T(8,128)(2,1)S(1)}, u32[]{:S(2)}, u32[]{:S(2)}) collective-permute-start(bf16[4,2,4,16,256]{4,3,2,1,0:T(8,128)(2,1)} %get-tuple-element.74), channel_id=1, source_target_pairs={{0,8},{4,12},{8,0},{12,4},{1,9},{5,13},{9,1},{13,5},{2,10},{6,14},... | collective-permute-start | bytes 786440 | tf_op jit(solution)/shard_map/ppermute | solution.py:561
  545.6 22.8 %collective-permute-start.25 = (bf16[4,2,4,16,256]{4,3,2,1,0:T(8,128)(2,1)}, bf16[4,2,4,16,256]{4,3,2,1,0:T(8,128)(2,1)S(1)}, u32[]{:S(2)}, u32[]{:S(2)}) collective-permute-start(bf16[4,2,4,16,256]{4,3,2,1,0:T(8,128)(2,1)} %get-tuple-element.80), channel_id=1, source_target_pairs={{0,4},{4,0},{8,12},{12,8},{1,5},{5,1},{9,13},{13,9},{2,6},{6,2},{1... | collective-permute-start | bytes 786440 | tf_op jit(solution)/shard_map/ppermute | solution.py:561
  556.7 29.8 %all-to-all-start.13 = ((bf16[8,2,2,4,16,256]{5,4,3,2,1,0:T(8,128)(2,1)}), bf16[8,2,2,4,16,256]{5,4,3,2,1,0:T(8,128)(2,1)S(1)}, u32[]{:S(2)}, u32[]{:S(2)}) async-start(bf16[8,2,2,4,16,256]{5,4,3,2,1,0:T(8,128)(2,1)} %bitcast.47), calls=%async_computation.13 | async-start | bytes 2097152 | tf_op jit(solution)/shard_map/all_to_all | solution.py:557
  561.7 23.2 %collective-permute-start.26 = (bf16[4,2,4,16,256]{4,3,2,1,0:T(8,128)(2,1)}, bf16[4,2,4,16,256]{4,3,2,1,0:T(8,128)(2,1)S(1)}, u32[]{:S(2)}, u32[]{:S(2)}) collective-permute-start(bf16[4,2,4,16,256]{4,3,2,1,0:T(8,128)(2,1)} %get-tuple-element.81), channel_id=1, source_target_pairs={{0,8},{4,12},{8,0},{12,4},{1,9},{5,13},{9,1},{13,5},{2,10},{6,14},... | collective-permute-start | bytes 786440 | tf_op jit(solution)/shard_map/ppermute | solution.py:561
  (43 other events, 503.6 us)
